TPU v7x, 128 devices: a whole 4x4x4 slice. The times are simulated.
128 devices in a mesh: gx: 16 (over z, x), gy: 8 (over y, core).
Axes of the slice: x: 4, y: 4, z: 4, core: 2. Of those that a mesh axis runs over, the one named last changes fastest.
Arguments:
- normals: float32 [16384, 2, 256], P(('gx', 'gy')), may hold values from -24 to 24
- fractions: float32 [16384, 2, 256], P(('gx', 'gy')), may hold values from 0.01 to 0.99
- offsets: int32 [16384, 256], P(('gx', 'gy')), may hold values from 0 to 8062, as said below
- owner: int32 [16384, 1], P(('gx', 'gy')), may hold values from 0 to 127; in each aligned block of 128 rows (0 to 127, 128 to 255, ...) at most 2 rows name the same one
- brick: int32 [16384], P(('gx', 'gy')), may hold values from 0 to 31
- fill: int32 [16384], P(('gx', 'gy')), may hold values from 1 to 256, 2621440 in all
Outputs:
- indicator: float32 [8, 2048, 2048], P('gy', None, 'gx')
- gradient: float32 [2, 8, 2048, 2048], P(None, 'gy', None, 'gx')
Inputs may be any that keep to these rules, and one draw needn't show every extreme that they name: Among the blocks held by one device no owner is named by more than 2 blocks. `offsets`: each offset is (iz * 8 + iy) * 128 + ix with iz below 8, iy at most 6 and ix at most 126; of the 256 points of one block, live or padding, no plane holds more than 64, and every block has one plane with exactly 64. Points of a block at positions from its fill on are padding.
All inputs are finite; a program needn't handle non-finite values.
Results may differ from a plain program's by a relative error of at most 0.0023.
Values sent between devices are 32-bit elements; how exact they have to be, the bound alone decides.
No kernel may reach another device: no remote copies, remote signals or barrier semaphores. Data moves between devices by JAX's collectives and lax.ppermute only.
A program may use at most 64 MiB of HBM per device.

v0:
```python
import math

import jax
import jax.numpy as jnp
from jax import lax
from jax.sharding import PartitionSpec as P

NX = 2048
NY = 2048
Z = 8
BX = 128
BY = 8


ALPHA = 4e-06


def passed_along(value, axis, steps):
    count = lax.axis_size(axis)
    pairs = [(source, (source + steps) % count) for source in range(count)]
    return lax.ppermute(value, axis, pairs)


def angles(row_count, col_count, modulus, direction):
    row_ids = lax.broadcasted_iota(jnp.int32, (row_count, col_count), 0)
    col_ids = lax.broadcasted_iota(jnp.int32, (row_count, col_count), 1)
    phase_angle = (row_ids * col_ids % modulus).astype(jnp.float32) * (2.0 * math.pi / modulus)
    return (jnp.cos(phase_angle), direction * jnp.sin(phase_angle))


def contract(values, matrix, position):
    letters = "abcdefgh"[: values.ndim]
    target = letters[:position] + "z" + letters[position + 1 :]
    return jnp.einsum(
        letters + "," + letters[position] + "z->" + target,
        values,
        matrix,
        precision=lax.Precision.HIGHEST,
    )


def rotate(real_part, imag_part, tables, position):
    cosine, sine_part = tables
    if imag_part is None:
        return (contract(real_part, cosine, position), contract(real_part, sine_part, position))
    new_real = contract(real_part, cosine, position) - contract(imag_part, sine_part, position)
    new_imag = contract(real_part, sine_part, position) + contract(imag_part, cosine, position)
    return (new_real, new_imag)


def twiddle(real_part, imag_part, tables, twist_shape):
    cosine = tables[0].reshape(twist_shape)
    sine_part = tables[1].reshape(twist_shape)
    return (real_part * cosine - imag_part * sine_part, real_part * sine_part + imag_part * cosine)


def split_len(length):
    inner_len = min(128, length)
    return (length // inner_len, inner_len)


def forward_local(real_part, imag_part, position, length):
    outer_len, inner_len = split_len(length)
    real_part, imag_part = rotate(
        real_part, imag_part, angles(outer_len, outer_len, outer_len, -1.0), position
    )
    twist_shape = [1] * real_part.ndim
    twist_shape[position] = outer_len
    twist_shape[position + 1] = inner_len
    real_part, imag_part = twiddle(
        real_part, imag_part, angles(outer_len, inner_len, length, -1.0), tuple(twist_shape)
    )
    cosine, sine_part = angles(inner_len, inner_len, inner_len, -1.0)
    return rotate(real_part, imag_part, (cosine, sine_part), position + 1)


def inverse_local(real_part, imag_part, position, length):
    outer_len, inner_len = split_len(length)
    present = real_part.shape[position + 1]
    cosine, sine_part = angles(inner_len, inner_len, inner_len, 1.0)
    real_part, imag_part = rotate(
        real_part, imag_part, (cosine[:present], sine_part[:present]), position + 1
    )
    twist_shape = [1] * real_part.ndim
    twist_shape[position] = outer_len
    twist_shape[position + 1] = inner_len
    real_part, imag_part = twiddle(
        real_part, imag_part, angles(outer_len, inner_len, length, 1.0), tuple(twist_shape)
    )
    return rotate(real_part, imag_part, angles(outer_len, outer_len, outer_len, 1.0), position)


def splat_blocks(payload, block_meta):
    group_size = payload.shape[0]
    points = payload.shape[2]
    live_mask = (
        lax.broadcasted_iota(jnp.int32, (group_size, points), 1) < block_meta[:, 1:2]
    ).astype(jnp.float32)
    normal_x = payload[:, 0] * live_mask
    normal_y = payload[:, 1] * live_mask
    frac_x = payload[:, 2]
    frac_y = payload[:, 3]
    cells = payload[:, 4].astype(jnp.int32)
    plane_ids = cells // (BY * BX)
    inside = cells % (BY * BX)
    row_ids = inside // BX
    col_ids = inside % BX
    grid_rows = lax.broadcasted_iota(jnp.int32, (1, Z * BY, 1), 1)
    same_plane = grid_rows // BY == plane_ids[:, None, :]
    local_row = grid_rows % BY
    lower_row = (same_plane & (local_row == row_ids[:, None, :])).astype(jnp.float32)
    upper_row = (same_plane & (local_row == row_ids[:, None, :] + 1)).astype(jnp.float32)
    left_side = jnp.concatenate(
        [
            normal_x[:, None, :]
            * (lower_row * (1.0 - frac_y[:, None, :]) + upper_row * frac_y[:, None, :]),
            normal_y[:, None, :] * (lower_row - upper_row),
        ],
        axis=2,
    )
    grid_cols = lax.broadcasted_iota(jnp.int32, (1, 1, BX), 2)
    lower_col = (grid_cols == col_ids[:, :, None]).astype(jnp.float32)
    upper_col = (grid_cols == col_ids[:, :, None] + 1).astype(jnp.float32)
    right_side = jnp.concatenate(
        [
            lower_col - upper_col,
            lower_col * (1.0 - frac_x[:, :, None]) + upper_col * frac_x[:, :, None],
        ],
        axis=1,
    )
    return jnp.einsum("grp,gpc->grc", left_side, right_side, precision=lax.Precision.HIGHEST)


def shards(normals, fractions, offsets, owner, brick, fill):
    count_gx = lax.axis_size("gx")
    count_gy = lax.axis_size("gy")
    devices = count_gx * count_gy
    held_blocks = normals.shape[0]
    points = normals.shape[2]
    capacity = max(2, 2 * held_blocks // devices)
    total_slots = devices * capacity
    width_x = NX // count_gx
    width_y = NY // count_gy
    planes_group = Z // count_gy
    outer_y, inner_y = split_len(width_y)
    outer_x, inner_x = split_len(width_x)
    bricks_x = width_x // BX
    bricks_y = width_y // BY
    targets = owner[:, 0]
    row_ids = lax.broadcasted_iota(jnp.int32, (held_blocks, held_blocks), 0)
    col_ids = lax.broadcasted_iota(jnp.int32, (held_blocks, held_blocks), 1)
    earlier = (targets[:, None] == targets[None, :]) & (col_ids < row_ids)
    slot_ids = targets * capacity + jnp.sum(earlier.astype(jnp.int32), axis=1)
    payload = jnp.concatenate([normals, fractions, offsets.astype(jnp.float32)[:, None, :]], axis=1)
    block_meta = jnp.stack([brick, fill], axis=1).astype(jnp.float32)
    send_payload = jnp.zeros((total_slots, 5, points), jnp.float32).at[slot_ids].set(payload)
    send_meta = jnp.zeros((total_slots, 2), jnp.float32).at[slot_ids].set(block_meta)
    recv_payload, recv_meta = (
        lax.all_to_all(send_payload, ("gx", "gy"), split_axis=0, concat_axis=0, tiled=True),
        lax.all_to_all(send_meta, ("gx", "gy"), split_axis=0, concat_axis=0, tiled=True),
    )
    recv_meta = recv_meta.astype(jnp.int32)
    group_size = math.gcd(total_slots, 32)
    rounds = total_slots // group_size

    def accumulate(totals, pieces):
        brick_tiles = splat_blocks(pieces[0], pieces[1])
        return (totals.at[pieces[1][:, 0]].add(brick_tiles), None)

    start_tiles = jnp.zeros((bricks_x * bricks_y, Z * BY, BX), jnp.float32)
    stacked = (
        recv_payload.reshape(rounds, group_size, 5, points),
        recv_meta.reshape(rounds, group_size, 2),
    )
    brick_sums, unused = lax.scan(accumulate, start_tiles, stacked)
    grid = brick_sums.reshape(bricks_y, bricks_x, Z, BY, BX).transpose(2, 0, 3, 1, 4)
    grid = grid.reshape(count_gy, planes_group, width_y, width_x)
    planes_block = lax.all_to_all(grid, "gy", split_axis=0, concat_axis=0, tiled=True)
    item_count = planes_block.shape[3]
    real_part, imag_part = rotate(planes_block, None, angles(count_gy, count_gy, count_gy, -1.0), 0)
    real_part = real_part.reshape(count_gy, planes_group, outer_y, inner_y, item_count)
    imag_part = imag_part.reshape(count_gy, planes_group, outer_y, inner_y, item_count)
    real_part, imag_part = twiddle(
        real_part,
        imag_part,
        angles(count_gy, width_y, NY, -1.0),
        (count_gy, 1, outer_y, inner_y, 1),
    )
    row_real, row_imag = forward_local(real_part, imag_part, 2, width_y)
    row_real = row_real.reshape(count_gy, planes_group, outer_y, inner_y, 1, width_x)
    row_imag = row_imag.reshape(count_gy, planes_group, outer_y, inner_y, 1, width_x)
    col_real = lax.all_to_all(row_real, "gx", split_axis=3, concat_axis=4, tiled=True)
    col_imag = lax.all_to_all(row_imag, "gx", split_axis=3, concat_axis=4, tiled=True)
    col_real, col_imag = rotate(col_real, col_imag, angles(count_gx, count_gx, count_gx, -1.0), 4)
    full_shape = col_real.shape[:5] + (outer_x, inner_x)
    col_real = col_real.reshape(full_shape)
    col_imag = col_imag.reshape(full_shape)
    col_real, col_imag = twiddle(
        col_real,
        col_imag,
        angles(count_gx, width_x, NX, -1.0),
        (1, 1, 1, 1, count_gx, outer_x, inner_x),
    )
    freq_real, freq_imag = forward_local(col_real, col_imag, 5, width_x)
    block_cols = freq_real.shape[3]
    shape_y = (count_gy, 1, outer_y, block_cols, 1, 1, 1)
    shape_x = (1, 1, 1, 1, count_gx, outer_x, inner_x)
    high_y = lax.broadcasted_iota(jnp.int32, shape_y, 3) + lax.axis_index("gx") * block_cols
    freq_y = lax.broadcasted_iota(jnp.int32, shape_y, 0) + count_gy * (
        lax.broadcasted_iota(jnp.int32, shape_y, 2) + outer_y * high_y
    )
    freq_x = lax.broadcasted_iota(jnp.int32, shape_x, 4) + count_gx * (
        lax.broadcasted_iota(jnp.int32, shape_x, 5)
        + outer_x * lax.broadcasted_iota(jnp.int32, shape_x, 6)
    )
    part_x = -4.0 * jnp.square(
        jnp.sin(math.pi * jnp.minimum(freq_x, NX - freq_x).astype(jnp.float32) / NX)
    )
    part_y = -4.0 * jnp.square(
        jnp.sin(math.pi * jnp.minimum(freq_y, NY - freq_y).astype(jnp.float32) / NY)
    )
    operator_symbol = part_x + part_y - ALPHA
    nyquist = (freq_x == NX // 2) | (freq_y == NY // 2)
    response = jnp.where(nyquist, 0.0, 1.0 / operator_symbol) / (NX * NY)
    freq_real = freq_real * response
    freq_imag = freq_imag * response
    back_real, back_imag = inverse_local(freq_real, freq_imag, 5, width_x)
    back_real, back_imag = twiddle(
        back_real,
        back_imag,
        angles(count_gx, width_x, NX, 1.0),
        (1, 1, 1, 1, count_gx, outer_x, inner_x),
    )
    back_real, back_imag = rotate(
        back_real, back_imag, angles(count_gx, count_gx, count_gx, 1.0), 4
    )
    back_real = back_real.reshape(count_gy, planes_group, outer_y, block_cols, count_gx, width_x)
    back_imag = back_imag.reshape(count_gy, planes_group, outer_y, block_cols, count_gx, width_x)
    inv_real = lax.all_to_all(back_real, "gx", split_axis=4, concat_axis=3, tiled=True)
    inv_imag = lax.all_to_all(back_imag, "gx", split_axis=4, concat_axis=3, tiled=True)
    inv_real, inv_imag = inverse_local(inv_real, inv_imag, 2, width_y)
    inv_real, inv_imag = twiddle(
        inv_real,
        inv_imag,
        angles(count_gy, width_y, NY, 1.0),
        (count_gy, 1, outer_y, inner_y, 1, 1),
    )
    cosine, sine_part = angles(count_gy, count_gy, count_gy, 1.0)
    field = contract(inv_real, cosine, 0) - contract(inv_imag, sine_part, 0)
    indicator = (
        field.reshape(count_gy, planes_group, width_y, width_x)
        .transpose(1, 0, 2, 3)
        .reshape(planes_group, NY, width_x)
    )
    ahead = passed_along(indicator[:, :, :1], "gx", -1)
    grad_x = jnp.concatenate([indicator[:, :, 1:], ahead], axis=2) - indicator
    grad_y = jnp.roll(indicator, -1, axis=1) - indicator
    return (indicator, jnp.stack([grad_x, grad_y]))


def solution(mesh):
    in_specs = (
        P(("gx", "gy"), None, None),
        P(("gx", "gy"), None, None),
        P(("gx", "gy"), None),
        P(("gx", "gy"), None),
        P(("gx", "gy")),
        P(("gx", "gy")),
    )
    out_specs = (P("gy", None, "gx"), P(None, "gy", None, "gx"))
    return jax.shard_map(shards, mesh=mesh, in_specs=in_specs, out_specs=out_specs, check_vma=False)
```

profile of v0, /device:TPU:0, one launch (start us, length us, event | category | flops | bytes accessed | tf_op | source)
XLA Modules:
  0.0 365.2 jit_solution(7617602384847698073)
XLA Ops:
  5.4 11.2 %all-to-all-start = ((f32[128,2,2]{1,2,0:T(2,128)}), f32[128,2,2]{1,2,0:T(2,128)S(1)}, u32[]{:S(2)}, u32[]{:S(2)}) async-start(f32[128,2,2]{1,2,0:T(2,128)} %copy.220), calls=%async_computation | async-start | bytes 262144 | tf_op jit(solution)/shard_map/all_to_all | solution.py:160
  20.5 13.7 %scatter_fusion.1 = f32[256,5,256]{2,1,0:T(8,128)} fusion(f32[256,5,256]{2,1,0:T(8,128)} %broadcast_in_dim.13, s32[128]{0:T(128)S(1)} %fusion.224, f32[128,5,256]{2,1,0:T(8,128)S(1)} %pad_maximum_fusion.1), kind=kCustom, calls=%fused_computation.2 | custom fusion | bytes 1966592 | tf_op jit(solution)/shard_map/scatter | solution.py:156
  34.2 10.3 %all-to-all-start.1 = ((f32[256,5,256]{2,1,0:T(8,128)}), f32[256,5,256]{2,1,0:T(8,128)S(1)}, u32[]{:S(2)}, u32[]{:S(2)}) async-start(f32[256,5,256]{2,1,0:T(8,128)} %scatter_fusion.1), calls=%async_computation.1 | async-start | bytes 4194304 | tf_op jit(solution)/shard_map/all_to_all | solution.py:159
  44.9 30.0 %all-to-all-done.1 = f32[256,5,256]{2,1,0:T(8,128)S(1)} async-done(((f32[256,5,256]{2,1,0:T(8,128)}), f32[256,5,256]{2,1,0:T(8,128)S(1)}, u32[]{:S(2)}, u32[]{:S(2)}) %all-to-all-start.1) | async-done | bytes 1310752 | tf_op jit(solution)/shard_map/all_to_all | solution.py:159
  75.4 108.3 %while.13 = (s32[]{:T(128)}, f32[32,64,128]{2,1,0:T(8,128)S(1)}, s32[8,32,2]{1,0,2:T(8,128)S(1)}, f32[8,32,5,256]{3,1,2,0:T(8,128)S(1)}, s32[]{:T(128)}) while((s32[]{:T(128)}, f32[32,64,128]{2,1,0:T(8,128)S(1)}, s32[8,32,2]{1,0,2:T(8,128)S(1)}, f32[8,32,5,256]{3,1,2,0:T(8,128)S(1)}, s32[]{:T(128)}) %tuple.75), condition=%wide.region_5.6_spmd, body=%wide.region_3.5_spmd.sunk | while | flops 1629815680 | bytes 30689604 | solution.py:175
  77.0 4.5 %convert_subtract_fusion.2 = (f32[32,256,128]{2,1,0:T(8,128)S(1)}, f32[32,256,128]{2,1,0:T(8,128)S(1)}) fusion(s32[32,256]{1,0:T(8,128)S(1)} %get-tuple-element.205, s32[32,256]{1,0:T(8,128)S(1)} %get-tuple-element.206, f32[32,256]{1,0:T(8,128)S(1)} %get-tuple-element.208, f32[32,256]{1,0:T(8,128)S(1)} %broadcast_subtract_fusion.2), kind=kLoop, calls=%fused_computation.11.clone.1 | loop fusion | flops 8388608 | bytes 8519680 | tf_op jit(solution)/shard_map/while/body/eval_jaxpr/sub | solution.py:126
  81.4 5.3 %fusion.425 = f32[32,64,128]{2,1,0:T(8,128)S(1)} fusion(f32[32,256,128]{2,1,0:T(8,128)S(1)} %get-tuple-element.209, f32[32,256,128]{2,1,0:T(8,128)S(1)} %get-tuple-element.210, f32[32,64,256]{2,1,0:T(8,128)S(1)} %get-tuple-element.221, f32[32,64,256]{2,1,0:T(8,128)S(1)} %get-tuple-element.222), kind=kOutput, calls=%fused_computation.3.clone.1 | convolution fusion | flops 1613758464 | bytes 13631488 | tf_op jit(solution)/shard_map/while/body/eval_jaxpr/grp,gpc->grc/dot_general | solution.py:131
  90.5 4.5 %convert_subtract_fusion.2 = (f32[32,256,128]{2,1,0:T(8,128)S(1)}, f32[32,256,128]{2,1,0:T(8,128)S(1)}) fusion(s32[32,256]{1,0:T(8,128)S(1)} %get-tuple-element.205, s32[32,256]{1,0:T(8,128)S(1)} %get-tuple-element.206, f32[32,256]{1,0:T(8,128)S(1)} %get-tuple-element.208, f32[32,256]{1,0:T(8,128)S(1)} %broadcast_subtract_fusion.2), kind=kLoop, calls=%fused_computation.11.clone.1 | loop fusion | flops 8388608 | bytes 8519680 | tf_op jit(solution)/shard_map/while/body/eval_jaxpr/sub | solution.py:126
  95.0 5.3 %fusion.425 = f32[32,64,128]{2,1,0:T(8,128)S(1)} fusion(f32[32,256,128]{2,1,0:T(8,128)S(1)} %get-tuple-element.209, f32[32,256,128]{2,1,0:T(8,128)S(1)} %get-tuple-element.210, f32[32,64,256]{2,1,0:T(8,128)S(1)} %get-tuple-element.221, f32[32,64,256]{2,1,0:T(8,128)S(1)} %get-tuple-element.222), kind=kOutput, calls=%fused_computation.3.clone.1 | convolution fusion | flops 1613758464 | bytes 13631488 | tf_op jit(solution)/shard_map/while/body/eval_jaxpr/grp,gpc->grc/dot_general | solution.py:131
  104.0 4.5 %convert_subtract_fusion.2 = (f32[32,256,128]{2,1,0:T(8,128)S(1)}, f32[32,256,128]{2,1,0:T(8,128)S(1)}) fusion(s32[32,256]{1,0:T(8,128)S(1)} %get-tuple-element.205, s32[32,256]{1,0:T(8,128)S(1)} %get-tuple-element.206, f32[32,256]{1,0:T(8,128)S(1)} %get-tuple-element.208, f32[32,256]{1,0:T(8,128)S(1)} %broadcast_subtract_fusion.2), kind=kLoop, calls=%fused_computation.11.clone.1 | loop fusion | flops 8388608 | bytes 8519680 | tf_op jit(solution)/shard_map/while/body/eval_jaxpr/sub | solution.py:126
  108.5 5.3 %fusion.425 = f32[32,64,128]{2,1,0:T(8,128)S(1)} fusion(f32[32,256,128]{2,1,0:T(8,128)S(1)} %get-tuple-element.209, f32[32,256,128]{2,1,0:T(8,128)S(1)} %get-tuple-element.210, f32[32,64,256]{2,1,0:T(8,128)S(1)} %get-tuple-element.221, f32[32,64,256]{2,1,0:T(8,128)S(1)} %get-tuple-element.222), kind=kOutput, calls=%fused_computation.3.clone.1 | convolution fusion | flops 1613758464 | bytes 13631488 | tf_op jit(solution)/shard_map/while/body/eval_jaxpr/grp,gpc->grc/dot_general | solution.py:131
  117.6 4.5 %convert_subtract_fusion.2 = (f32[32,256,128]{2,1,0:T(8,128)S(1)}, f32[32,256,128]{2,1,0:T(8,128)S(1)}) fusion(s32[32,256]{1,0:T(8,128)S(1)} %get-tuple-element.205, s32[32,256]{1,0:T(8,128)S(1)} %get-tuple-element.206, f32[32,256]{1,0:T(8,128)S(1)} %get-tuple-element.208, f32[32,256]{1,0:T(8,128)S(1)} %broadcast_subtract_fusion.2), kind=kLoop, calls=%fused_computation.11.clone.1 | loop fusion | flops 8388608 | bytes 8519680 | tf_op jit(solution)/shard_map/while/body/eval_jaxpr/sub | solution.py:126
  122.1 5.3 %fusion.425 = f32[32,64,128]{2,1,0:T(8,128)S(1)} fusion(f32[32,256,128]{2,1,0:T(8,128)S(1)} %get-tuple-element.209, f32[32,256,128]{2,1,0:T(8,128)S(1)} %get-tuple-element.210, f32[32,64,256]{2,1,0:T(8,128)S(1)} %get-tuple-element.221, f32[32,64,256]{2,1,0:T(8,128)S(1)} %get-tuple-element.222), kind=kOutput, calls=%fused_computation.3.clone.1 | convolution fusion | flops 1613758464 | bytes 13631488 | tf_op jit(solution)/shard_map/while/body/eval_jaxpr/grp,gpc->grc/dot_general | solution.py:131
  131.1 4.5 %convert_subtract_fusion.2 = (f32[32,256,128]{2,1,0:T(8,128)S(1)}, f32[32,256,128]{2,1,0:T(8,128)S(1)}) fusion(s32[32,256]{1,0:T(8,128)S(1)} %get-tuple-element.205, s32[32,256]{1,0:T(8,128)S(1)} %get-tuple-element.206, f32[32,256]{1,0:T(8,128)S(1)} %get-tuple-element.208, f32[32,256]{1,0:T(8,128)S(1)} %broadcast_subtract_fusion.2), kind=kLoop, calls=%fused_computation.11.clone.1 | loop fusion | flops 8388608 | bytes 8519680 | tf_op jit(solution)/shard_map/while/body/eval_jaxpr/sub | solution.py:126
  135.6 5.3 %fusion.425 = f32[32,64,128]{2,1,0:T(8,128)S(1)} fusion(f32[32,256,128]{2,1,0:T(8,128)S(1)} %get-tuple-element.209, f32[32,256,128]{2,1,0:T(8,128)S(1)} %get-tuple-element.210, f32[32,64,256]{2,1,0:T(8,128)S(1)} %get-tuple-element.221, f32[32,64,256]{2,1,0:T(8,128)S(1)} %get-tuple-element.222), kind=kOutput, calls=%fused_computation.3.clone.1 | convolution fusion | flops 1613758464 | bytes 13631488 | tf_op jit(solution)/shard_map/while/body/eval_jaxpr/grp,gpc->grc/dot_general | solution.py:131
  144.6 4.5 %convert_subtract_fusion.2 = (f32[32,256,128]{2,1,0:T(8,128)S(1)}, f32[32,256,128]{2,1,0:T(8,128)S(1)}) fusion(s32[32,256]{1,0:T(8,128)S(1)} %get-tuple-element.205, s32[32,256]{1,0:T(8,128)S(1)} %get-tuple-element.206, f32[32,256]{1,0:T(8,128)S(1)} %get-tuple-element.208, f32[32,256]{1,0:T(8,128)S(1)} %broadcast_subtract_fusion.2), kind=kLoop, calls=%fused_computation.11.clone.1 | loop fusion | flops 8388608 | bytes 8519680 | tf_op jit(solution)/shard_map/while/body/eval_jaxpr/sub | solution.py:126
  149.1 5.3 %fusion.425 = f32[32,64,128]{2,1,0:T(8,128)S(1)} fusion(f32[32,256,128]{2,1,0:T(8,128)S(1)} %get-tuple-element.209, f32[32,256,128]{2,1,0:T(8,128)S(1)} %get-tuple-element.210, f32[32,64,256]{2,1,0:T(8,128)S(1)} %get-tuple-element.221, f32[32,64,256]{2,1,0:T(8,128)S(1)} %get-tuple-element.222), kind=kOutput, calls=%fused_computation.3.clone.1 | convolution fusion | flops 1613758464 | bytes 13631488 | tf_op jit(solution)/shard_map/while/body/eval_jaxpr/grp,gpc->grc/dot_general | solution.py:131
  158.2 4.5 %convert_subtract_fusion.2 = (f32[32,256,128]{2,1,0:T(8,128)S(1)}, f32[32,256,128]{2,1,0:T(8,128)S(1)}) fusion(s32[32,256]{1,0:T(8,128)S(1)} %get-tuple-element.205, s32[32,256]{1,0:T(8,128)S(1)} %get-tuple-element.206, f32[32,256]{1,0:T(8,128)S(1)} %get-tuple-element.208, f32[32,256]{1,0:T(8,128)S(1)} %broadcast_subtract_fusion.2), kind=kLoop, calls=%fused_computation.11.clone.1 | loop fusion | flops 8388608 | bytes 8519680 | tf_op jit(solution)/shard_map/while/body/eval_jaxpr/sub | solution.py:126
  162.6 5.3 %fusion.425 = f32[32,64,128]{2,1,0:T(8,128)S(1)} fusion(f32[32,256,128]{2,1,0:T(8,128)S(1)} %get-tuple-element.209, f32[32,256,128]{2,1,0:T(8,128)S(1)} %get-tuple-element.210, f32[32,64,256]{2,1,0:T(8,128)S(1)} %get-tuple-element.221, f32[32,64,256]{2,1,0:T(8,128)S(1)} %get-tuple-element.222), kind=kOutput, calls=%fused_computation.3.clone.1 | convolution fusion | flops 1613758464 | bytes 13631488 | tf_op jit(solution)/shard_map/while/body/eval_jaxpr/grp,gpc->grc/dot_general | solution.py:131
  171.7 4.5 %convert_subtract_fusion.2 = (f32[32,256,128]{2,1,0:T(8,128)S(1)}, f32[32,256,128]{2,1,0:T(8,128)S(1)}) fusion(s32[32,256]{1,0:T(8,128)S(1)} %get-tuple-element.205, s32[32,256]{1,0:T(8,128)S(1)} %get-tuple-element.206, f32[32,256]{1,0:T(8,128)S(1)} %get-tuple-element.208, f32[32,256]{1,0:T(8,128)S(1)} %broadcast_subtract_fusion.2), kind=kLoop, calls=%fused_computation.11.clone.1 | loop fusion | flops 8388608 | bytes 8519680 | tf_op jit(solution)/shard_map/while/body/eval_jaxpr/sub | solution.py:126
  176.2 5.3 %fusion.425 = f32[32,64,128]{2,1,0:T(8,128)S(1)} fusion(f32[32,256,128]{2,1,0:T(8,128)S(1)} %get-tuple-element.209, f32[32,256,128]{2,1,0:T(8,128)S(1)} %get-tuple-element.210, f32[32,64,256]{2,1,0:T(8,128)S(1)} %get-tuple-element.221, f32[32,64,256]{2,1,0:T(8,128)S(1)} %get-tuple-element.222), kind=kOutput, calls=%fused_computation.3.clone.1 | convolution fusion | flops 1613758464 | bytes 13631488 | tf_op jit(solution)/shard_map/while/body/eval_jaxpr/grp,gpc->grc/dot_general | solution.py:131
  189.2 15.1 %all-to-all-done.2 = f32[8,1,256,128]{3,2,1,0:T(8,128)S(1)} async-done(((f32[8,1,256,128]{3,2,1,0:T(8,128)}), f32[8,1,256,128]{3,2,1,0:T(8,128)S(1)}, u32[]{:S(2)}, u32[]{:S(2)}) %all-to-all-start.2) | async-done | bytes 1048608 | tf_op jit(solution)/shard_map/all_to_all | solution.py:178
  211.4 3.9 %fusion.71 = f32[2,8,128,128]{3,0,2,1:T(2,128)S(1)} fusion(f32[8,2,128,128]{3,0,2,1:T(8,128)S(1)} %get-tuple-element.144), kind=kOutput, calls=%fused_computation.164 | convolution fusion | flops 6291516 | bytes 2097152 | tf_op jit(solution)/shard_map/abcde,cz->abzde/dot_general | solution.py:34
  215.3 4.0 %fusion.32 = f32[2,8,1,128,128]{4,0,3,1,2:T(2,128)S(1)} fusion(f32[2,8,128,128]{3,0,2,1:T(2,128)S(1)} %fusion.73, f32[8,2,128,128]{3,0,2,1:T(8,128)S(1)} %get-tuple-element.143), kind=kOutput, calls=%fused_computation.97 | convolution fusion | flops 6553660 | bytes 3145728 | tf_op jit(solution)/shard_map/abcde,cz->abzde/dot_general | solution.py:34
  219.3 5.7 %add_bitcast_fusion.3 = (f32[8,2,128,128]{3,1,2,0:T(2,128)S(1)}, f32[8,2,128,128]{3,1,2,0:T(2,128)S(1)}) fusion(f32[2,8,1,128,128]{4,0,3,1,2:T(2,128)S(1)} %fusion.32, f32[2,128]{0,1:T(8,128)S(1)} %copy.236, f32[2,128]{0,1:T(8,128)S(1)} %copy.233, f32[2,8,128,128]{3,0,2,1:T(2,128)S(1)} %fusion.71, f32[8,2,128,128]{3,0,2,1:T(8,128)S(1)} %get-tuple-element.143), kind=kOutput, calls=%fused_computation.138 | convolution fusion | flops 8126520 | bytes 5244928 | tf_op jit(solution)/shard_map/abcde,cz->abzde/dot_general | solution.py:34
  237.6 13.1 %all-to-all-done.3 = f32[8,1,2,128,1,128]{5,2,0,4,1,3:T(2,128)S(1)} async-done(((f32[8,1,2,128,1,128]{5,2,0,4,1,3:T(2,128)}), f32[8,1,2,128,1,128]{5,2,0,4,1,3:T(2,128)S(1)}, u32[]{:S(2)}, u32[]{:S(2)}) %all-to-all-start.3) | async-done | bytes 1048608 | tf_op jit(solution)/shard_map/all_to_all | solution.py:192
  250.7 4.1 %all-to-all-start.4 = ((f32[8,1,2,128,1,128]{5,2,0,4,1,3:T(2,128)}), f32[8,1,2,128,1,128]{5,2,0,4,1,3:T(2,128)S(1)}, u32[]{:S(2)}, u32[]{:S(2)}) async-start(f32[8,1,2,128,1,128]{5,2,0,4,1,3:T(2,128)} %copy.244), calls=%async_computation.4 | async-start | bytes 2097152 | tf_op jit(solution)/shard_map/all_to_all | solution.py:193
  259.1 11.5 %all-to-all-done.4 = f32[8,1,2,128,1,128]{5,2,0,4,1,3:T(2,128)S(1)} async-done(((f32[8,1,2,128,1,128]{5,2,0,4,1,3:T(2,128)}), f32[8,1,2,128,1,128]{5,2,0,4,1,3:T(2,128)S(1)}, u32[]{:S(2)}, u32[]{:S(2)}) %all-to-all-start.4) | async-done | bytes 1048608 | tf_op jit(solution)/shard_map/all_to_all | solution.py:193
  296.6 12.9 %all-to-all-done.5 = f32[8,1,2,8,16,128]{5,3,2,0,1,4:T(8,128)S(1)} async-done(((f32[8,1,2,8,16,128]{5,3,2,0,1,4:T(8,128)}), f32[8,1,2,8,16,128]{5,3,2,0,1,4:T(8,128)S(1)}, u32[]{:S(2)}, u32[]{:S(2)}) %all-to-all-start.5) | async-done | bytes 1048608 | tf_op jit(solution)/shard_map/all_to_all | solution.py:239
  319.1 10.7 %all-to-all-done.6 = f32[8,1,2,8,16,128]{5,3,2,0,1,4:T(8,128)S(1)} async-done(((f32[8,1,2,8,16,128]{5,3,2,0,1,4:T(8,128)}), f32[8,1,2,8,16,128]{5,3,2,0,1,4:T(8,128)S(1)}, u32[]{:S(2)}, u32[]{:S(2)}) %all-to-all-start.6) | async-done | bytes 1048608 | tf_op jit(solution)/shard_map/all_to_all | solution.py:240
  341.7 4.0 %fusion.29 = f32[8,1,2,128,1,128]{5,2,3,0,4,1:T(2,128)S(1)} fusion(f32[2,8,128,128]{3,0,2,1:T(2,128)S(1)} %fusion.65, f32[8,2,128,128]{3,2,1,0:T(8,128)S(1)} %get-tuple-element.149), kind=kOutput, calls=%fused_computation.91 | convolution fusion | flops 6553656 | bytes 3145728 | tf_op jit(solution)/shard_map/abcdef,cz->abzdef/dot_general | solution.py:34
  345.8 7.2 %add_bitcast_fusion.1 = (f32[8,2,128,128]{3,1,2,0:T(2,128)S(1)}, f32[8,2,128,128]{3,1,2,0:T(2,128)S(1)}) fusion(f32[8,1,2,128,1,128]{5,2,3,0,4,1:T(2,128)S(1)} %fusion.29, f32[8,2,128]{1,2,0:T(8,128)S(1)} %copy-done.2, f32[8,2,128]{1,2,0:T(8,128)S(1)} %copy-done.1, f32[2,8,128,128]{3,0,2,1:T(2,128)S(1)} %fusion.67, ...), kind=kOutput, calls=%fused_computation.123 | convolution fusion | flops 8126520 | bytes 5259264 | tf_op jit(solution)/shard_map/abcdef,cz->abzdef/dot_general | solution.py:34
  (183 shorter events, 127.4 us)
Async XLA Ops:
  5.4 28.8 %all-to-all-start = ((f32[128,2,2]{1,2,0:T(2,128)}), f32[128,2,2]{1,2,0:T(2,128)S(1)}, u32[]{:S(2)}, u32[]{:S(2)}) async-start(f32[128,2,2]{1,2,0:T(2,128)} %copy.220), calls=%async_computation | async-start | bytes 262144 | tf_op jit(solution)/shard_map/all_to_all | solution.py:160
  34.2 40.6 %all-to-all-start.1 = ((f32[256,5,256]{2,1,0:T(8,128)}), f32[256,5,256]{2,1,0:T(8,128)S(1)}, u32[]{:S(2)}, u32[]{:S(2)}) async-start(f32[256,5,256]{2,1,0:T(8,128)} %scatter_fusion.1), calls=%async_computation.1 | async-start | bytes 4194304 | tf_op jit(solution)/shard_map/all_to_all | solution.py:159
  184.7 19.6 %all-to-all-start.2 = ((f32[8,1,256,128]{3,2,1,0:T(8,128)}), f32[8,1,256,128]{3,2,1,0:T(8,128)S(1)}, u32[]{:S(2)}, u32[]{:S(2)}) async-start(f32[8,1,256,128]{3,2,1,0:T(8,128)} %copy_bitcast_fusion), calls=%async_computation.2 | async-start | bytes 2097152 | tf_op jit(solution)/shard_map/all_to_all | solution.py:178
  229.4 21.3 %all-to-all-start.3 = ((f32[8,1,2,128,1,128]{5,2,0,4,1,3:T(2,128)}), f32[8,1,2,128,1,128]{5,2,0,4,1,3:T(2,128)S(1)}, u32[]{:S(2)}, u32[]{:S(2)}) async-start(f32[8,1,2,128,1,128]{5,2,0,4,1,3:T(2,128)} %copy.239), calls=%async_computation.3 | async-start | bytes 2097152 | tf_op jit(solution)/shard_map/all_to_all | solution.py:192
  250.7 20.0 %all-to-all-start.4 = ((f32[8,1,2,128,1,128]{5,2,0,4,1,3:T(2,128)}), f32[8,1,2,128,1,128]{5,2,0,4,1,3:T(2,128)S(1)}, u32[]{:S(2)}, u32[]{:S(2)}) async-start(f32[8,1,2,128,1,128]{5,2,0,4,1,3:T(2,128)} %copy.244), calls=%async_computation.4 | async-start | bytes 2097152 | tf_op jit(solution)/shard_map/all_to_all | solution.py:193
  289.5 20.0 %all-to-all-start.5 = ((f32[8,1,2,8,16,128]{5,3,2,0,1,4:T(8,128)}), f32[8,1,2,8,16,128]{5,3,2,0,1,4:T(8,128)S(1)}, u32[]{:S(2)}, u32[]{:S(2)}) async-start(f32[8,1,2,8,16,128]{5,3,2,0,1,4:T(8,128)} %copy.257), calls=%async_computation.5 | async-start | bytes 2097152 | tf_op jit(solution)/shard_map/all_to_all | solution.py:239
  309.5 20.3 %all-to-all-start.6 = ((f32[8,1,2,8,16,128]{5,3,2,0,1,4:T(8,128)}), f32[8,1,2,8,16,128]{5,3,2,0,1,4:T(8,128)S(1)}, u32[]{:S(2)}, u32[]{:S(2)}) async-start(f32[8,1,2,8,16,128]{5,3,2,0,1,4:T(8,128)} %copy.259), calls=%async_computation.6 | async-start | bytes 2097152 | tf_op jit(solution)/shard_map/all_to_all | solution.py:240
  341.7 4.1 %copy-start.1 = (f32[8,2,128]{1,2,0:T(8,128)S(1)}, f32[8,2,128]{1,2,0:T(8,128)}, u32[]{:S(2)}) copy-start(f32[8,2,128]{1,2,0:T(8,128)} %copy.263) | copy-start | bytes 24580
  341.7 4.1 %copy-start.2 = (f32[8,2,128]{1,2,0:T(8,128)S(1)}, f32[8,2,128]{1,2,0:T(8,128)}, u32[]{:S(2)}) copy-start(f32[8,2,128]{1,2,0:T(8,128)} %copy.266) | copy-start | bytes 24580
  356.2 5.8 %copy-start = (f32[8,2,128,128]{3,2,1,0:T(8,128)}, f32[8,2,128,128]{3,2,1,0:T(8,128)S(1)}, u32[]{:S(2)}) copy-start(f32[8,2,128,128]{3,2,1,0:T(8,128)S(1)} %copy.269) | copy-start | bytes 3145732
  356.9 3.7 %collective-permute-start = (f32[1,2048,1]{1,2,0:T(1,128)S(1)}, f32[1,2048,1]{1,2,0:T(1,128)S(1)}, u32[]{:S(2)}, u32[]{:S(2)}) collective-permute-start(f32[1,2048,1]{1,2,0:T(1,128)S(1)} %copy.270), channel_id=1, source_target_pairs={{0,120},{8,0},{16,8},{24,16},{32,24},{40,32},{48,40},{56,48},{64,5... | collective-permute-start | bytes 24584 | tf_op jit(solution)/shard_map/ppermute | solution.py:21
where the time goes:
time: 369 us; the launch traced here: 365 us
  matrix products  121 us (33%)
  waiting for transfers between devices  95.5 us (26%)
  other arithmetic  72.9 us (20%)
  starting transfers between devices  41.9 us (11%)
  local copies, waits for them, and re-layouts  31.6 us (9%)
    dot_general x36, matrix products, contract(): jnp.einsum(letters + ',' + letters[position] + 'z->' + target, values, ma...  78.7 us
    dot_general x8, matrix products, splat_blocks(): jnp.einsum('grp,gpc->grc', left_side, right_side, precision=lax.Precision...  42.4 us
    sub x8, other arithmetic, splat_blocks(): lower_col - upper_col  35.9 us
    all_to_all x1, waiting for transfers between devices, shards(): lax.all_to_all(send_payload, ('gx', 'gy'), split_axis=0, concat_axis=0, t...  30 us
    scatter-add x8, other arithmetic, accumulate(): return (totals.at[pieces[1][:, 0]].add(brick_tiles), None)  17.1 us
    all_to_all x1, waiting for transfers between devices, shards(): lax.all_to_all(grid, 'gy', split_axis=0, concat_axis=0, tiled=True)  15.1 us
    scatter x1, local copies, waits for them, and re-layouts, shards(): jnp.zeros((total_slots, 5, points), jnp.float32).at[slot_ids].set(payload)  13.7 us
    all_to_all x1, waiting for transfers between devices, shards(): lax.all_to_all(row_real, 'gx', split_axis=3, concat_axis=4, tiled=True)  13.1 us
  transfers between devices with their start and end apart: 8, of which 7 were waited for; matrix products, arithmetic and copies ran while one was open for 10% of the time, Pallas kernels for 0%

commit v1 on v0

v1 whole, which is shorter than its diff:
```python
import functools
import math

import jax
import jax.numpy as jnp
import numpy as np
from jax import lax
from jax.experimental import pallas as pl
from jax.experimental.pallas import tpu as pltpu
from jax.sharding import PartitionSpec as P

NX = 2048
NY = 2048
Z = 8
BX = 128
BY = 8
P_SIZE = 256
GX = 16
GY = 8
DEV = GX * GY
ALPHA = 4e-06
SLOTS = 8
F32 = jnp.float32
BF16 = jnp.bfloat16
C1 = math.cos(math.pi / 8)
C2 = math.cos(math.pi / 4)
C3 = math.cos(3 * math.pi / 8)
INTERPRET = False


def np_split(values, parts):
    pieces = []
    rest = np.asarray(values, np.float64)
    for _ in range(parts):
        piece = rest.astype(BF16)
        pieces.append(piece)
        rest = rest - piece.astype(np.float64)
    return pieces


def slot_rows():
    ky = np.zeros((SLOTS, 256), np.int64)
    k2 = np.arange(128)
    half = np.arange(64)
    ky[0] = np.concatenate([16 * half, 16 * half, 8 + 16 * half, 8 + 16 * half])
    for slot in range(1, SLOTS):
        ky[slot] = np.concatenate([slot + 16 * k2, slot + 16 * k2])
    return ky


@functools.lru_cache(None)
def tables():
    ky = slot_rows()
    b = np.arange(128)
    fwd = np.zeros((SLOTS, 256, 256))
    weight = np.full((SLOTS, 256), 2.0 / NY)
    half = np.arange(64)
    for part in range(2):
        freq = part * 8 + 16 * half
        theta = 2 * np.pi * ((freq[:, None] * b[None, :]) % NY) / NY
        fwd[0, part * 128 : part * 128 + 64, part * 128 : part * 128 + 128] = np.cos(theta)
        fwd[0, part * 128 + 64 : part * 128 + 128, part * 128 : part * 128 + 128] = -np.sin(theta)
    weight[0, 0] = 1.0 / NY
    for slot in range(1, SLOTS):
        freq = slot + 16 * np.arange(128)
        theta = 2 * np.pi * ((freq[:, None] * b[None, :]) % NY) / NY
        cos, sin = np.cos(theta), np.sin(theta)
        fwd[slot] = np.block([[cos, sin], [-sin, cos]])
    inv = np.transpose(fwd, (0, 2, 1)) * weight[:, None, :]
    c = 4 * np.sin(np.pi * np.minimum(ky, NY - ky) / NY) ** 2 + ALPHA
    j = np.arange(1, 129)
    mu = 4 * np.sin(np.pi * j / 258) ** 2
    resp = -1.0 / (mu[None, None, :] + c[:, :, None])
    x = np.arange(128)
    sine = np.sqrt(2 / 129) * np.sin(np.pi * (x[:, None] + 1) * j[None, :] / 129)
    alt = ((-1.0) ** x) @ sine
    edge = np.zeros((8, 128))
    edge[0], edge[1], edge[2] = sine[0], sine[127], alt
    nyq = 1.0 / (-4.0 - c)
    root = np.sqrt(c * (c + 4))
    big = 1 + c / 2 + root / 2
    logr = -np.log(big)

    def green(n):
        n = n % NX
        return -(np.exp(logr * n) + np.exp(logr * (NX - n))) / (root * (1 - np.exp(logr * NX)))

    link0 = np.zeros((GX, SLOTS, 4, 256))
    link1 = np.zeros((GX, SLOTS, 4, 256))
    for n in range(GX):
        link0[n, :, 0] = -green(128 * n)
        link1[n, :, 0] = -green(128 * (n - 1) - 1) + (1.0 if n == 1 else 0.0)
        link0[n, :, 1] = -green(128 * (n + 1) + 1) + (1.0 if n == GX - 1 else 0.0)
        link1[n, :, 1] = -green(128 * n)
    fh, fm, fl = np_split(fwd, 3)
    ih, im = np_split(inv, 2)
    sh, sm, sl = np_split(sine, 3)
    ss = np.block([[sh, sm], [sh, sm]])
    s2 = np.concatenate([sl, sh], axis=0)
    eh, em, el = np_split(edge, 3)
    edges = np.concatenate([eh, eh, em, em, eh, el], axis=1)
    diff = np.concatenate([sine[:, 1:], np.zeros((128, 1))], axis=1) - sine
    back = np.concatenate([sine.T, np.concatenate([sine.T[:, 1:], np.zeros((128, 1))], axis=1) - sine.T], axis=1)
    bh, bm = np_split(back, 2)
    back1 = np.concatenate([bh, bh], axis=0)
    rank = np.zeros((4, 384))
    rank[0, 0:128] = sine[0]
    rank[1, 0:128] = sine[127]
    rank[2, 128:256] = alt
    rank[1, 256 + 127] = 1.0
    rank[2, 256 + 127] = -1.0
    rh, rm = np_split(rank, 2)
    ranks = np.concatenate([rh, rh, rm, np.zeros((4, 384), BF16)], axis=0)
    f = np.float32
    return dict(
        fh=fh, fm=fm, fl=fl, ih=ih, im=im, ss=ss, s2=s2, edges=edges, resp=resp.astype(f),
        nyq=nyq.reshape(SLOTS, 1, 256).astype(f), link0=link0.astype(f), link1=link1.astype(f),
        back1=back1, back2=bm, ranks=ranks,
    )


def split2(value):
    high = value.astype(BF16)
    return high, (value - high.astype(F32)).astype(BF16)


def split3(value):
    high = value.astype(BF16)
    rest = value - high.astype(F32)
    mid = rest.astype(BF16)
    return high, mid, (rest - mid.astype(F32)).astype(BF16)


def dot(left, right):
    return jnp.dot(left, right, preferred_element_type=F32)


def pack_kernel(owner, brick, fill, normals, fractions, offsets, send, counts):
    blocks = normals.shape[0]

    def clear(d, carry):
        counts[d] = 0
        send[d, 4] = jnp.full((4, 128), -1.0, F32)
        return carry

    lax.fori_loop(0, DEV, clear, 0, unroll=8)
    lane = lax.broadcasted_iota(jnp.int32, (2, 256), 1)
    row4 = lax.broadcasted_iota(jnp.int32, (4, 128), 0)

    def one(b, carry):
        d = owner[b]
        slot = counts[d]
        counts[d] = slot + 1
        live = jnp.where(lane < fill[b], normals[b], 0.0)
        frac = fractions[b]
        send[d, 2 * slot] = jnp.concatenate([live[:, :128], live[:, 128:]], axis=0)
        send[d, 2 * slot + 1] = jnp.concatenate(
            [frac[1:2, :128], frac[0:1, :128], frac[1:2, 128:], frac[0:1, 128:]], axis=0
        )
        cell = (offsets[pl.ds(b, 1), :] + brick[b] * (Z * BY * BX)).astype(F32)
        two = jnp.concatenate([cell[:, :128], cell[:, 128:]], axis=0)
        send[d, 4] = jnp.where(row4 // 2 == slot, jnp.concatenate([two, two], axis=0), send[d, 4])
        return carry

    lax.fori_loop(0, blocks, one, 0, unroll=4)


def splat_kernel(first, recv, out, acc):
    bricks = acc.shape[0]

    def clear(l, carry):
        acc[l] = jnp.zeros(acc.shape[1:], F32)
        return carry

    lax.fori_loop(0, bricks, clear, 0)
    rows = lax.broadcasted_iota(jnp.int32, (64, 128), 0)
    cols = lax.broadcasted_iota(jnp.int32, (128, 128), 0)

    def spread(row, matrix):
        return jnp.broadcast_to(row, matrix.shape)

    def one_slot(d, slot):
        cell2 = recv[d, 4][2 * slot : 2 * slot + 2].astype(jnp.int32)
        norm = recv[d, 2 * slot]
        frac = recv[d, 2 * slot + 1]
        filled = first[2 * d + slot] >= 0
        norm = jnp.where(filled, norm, 0.0)
        frac = jnp.where(filled, frac, 0.0)
        far = norm * frac
        near = norm * (1.0 - frac)
        near_h = near.astype(BF16).astype(F32)
        far_h = far.astype(BF16).astype(F32)
        near_l = near - near_h
        far_l = far - far_h
        line2 = (cell2 >> 7) & 63
        col2 = cell2 & 127
        high, low, right = [], [], []
        for half in range(2):
            line = spread(line2[half : half + 1], rows)
            here = line == rows
            below = line + 1 == rows
            x = 2 * half
            for parts, near_v, far_v in ((high, near_h, far_h), (low, near_l, far_l)):
                flux_x = jnp.where(
                    here,
                    spread(near_v[x : x + 1], rows),
                    jnp.where(below, spread(far_v[x : x + 1], rows), 0.0),
                )
                flux_y0 = jnp.where(here, spread(near_v[x + 1 : x + 2], rows), 0.0)
                flux_y1 = jnp.where(here, spread(far_v[x + 1 : x + 2], rows), 0.0)
                parts.append(
                    jnp.concatenate(
                        [flux_x.astype(BF16), flux_y0.astype(BF16), flux_y1.astype(BF16)], axis=0
                    )
                )
            right.append((spread(col2[half : half + 1], cols) == cols).astype(F32).astype(BF16))
        left = jnp.concatenate(high, axis=1)
        left_low = jnp.concatenate(low, axis=1)
        right = jnp.concatenate(right, axis=1)
        dims = (((1,), (1,)), ((), ()))
        piece = lax.dot_general(left, right, dims, preferred_element_type=F32)
        return piece + lax.dot_general(left_low, right, dims, preferred_element_type=F32)

    def one(d, carry):
        pieces = [one_slot(d, 0), one_slot(d, 1)]
        for slot in range(2):
            l = jnp.maximum(first[2 * d + slot], 0) >> 13
            acc[l] += pieces[slot]
        return carry

    lax.fori_loop(0, DEV, one, 0)

    def finish(l, carry):
        flux_x = acc[l, 0:64].reshape(Z, BY, 128)
        flux_y = (acc[l, 64:128] + pltpu.roll(acc[l, 128:192], 1, axis=1)).reshape(Z, BY, 128)
        moved_x = pltpu.roll(acc[l, 0:64], 1, axis=1).reshape(Z, BY, 128)
        tile = flux_x - moved_x + flux_y - pltpu.roll(flux_y, 1, axis=1)
        out[:, pl.ds(pl.multiple_of(l * BY, BY), BY), :] = tile
        return carry

    lax.fori_loop(0, bricks, finish, 0)


def radix_forward(f):
    e = [f[a] + f[a + 8] for a in range(8)]
    o = [f[a] - f[a + 8] for a in range(8)]
    p = [e[a] + e[a + 4] for a in range(4)]
    q = [e[a] - e[a + 4] for a in range(4)]
    even, odd = p[0] + p[2], p[1] + p[3]
    out = [None] * 8
    out[0] = (even + odd, even - odd)
    out[4] = (p[0] - p[2], p[3] - p[1])
    t1 = C2 * (q[1] - q[3])
    t2 = C2 * (q[1] + q[3])
    out[2] = (q[0] + t1, -(q[2] + t2))
    out[6] = (q[0] - t1, q[2] - t2)
    d = [None] + [o[a] - o[8 - a] for a in range(1, 4)]
    s = [None] + [o[a] + o[8 - a] for a in range(1, 4)]
    d2, s2 = C2 * d[2], C2 * s[2]
    base_p, base_m = o[0] + d2, o[0] - d2
    u1 = C1 * d[1] + C3 * d[3]
    u3 = C3 * d[1] - C1 * d[3]
    v1 = C3 * s[1] + C1 * s[3]
    v3 = C1 * s[1] - C3 * s[3]
    w_p, w_m = s2 + o[4], s2 - o[4]
    out[1] = (base_p + u1, -(v1 + w_p))
    out[7] = (base_p - u1, w_p - v1)
    out[3] = (base_m + u3, -(v3 + w_m))
    out[5] = (base_m - u3, w_m - v3)
    return out


def radix_inverse(h):
    (h0, h8) = h[0]
    plus, minus = h0 + h8, h0 - h8
    r4, i4 = h[4]
    part_a = [plus + r4, minus - i4, plus - r4, minus + i4]
    (r2, i2), (r6, i6) = h[2], h[6]
    dr, sr = r2 - r6, r2 + r6
    di, si = i2 - i6, i2 + i6
    part_b = [sr, C2 * (dr - si), -di, -C2 * (dr + si)]
    e = [part_a[a] + part_b[a] for a in range(4)] + [part_a[a] - part_b[a] for a in range(4)]
    (r1, i1), (r3, i3), (r5, i5), (r7, i7) = h[1], h[3], h[5], h[7]
    p17, m17, p35, m35 = r1 + r7, r1 - r7, r3 + r5, r3 - r5
    sums = [p17 + p35, C1 * m17 + C3 * m35, C2 * (p17 - p35), C3 * m17 - C1 * m35]
    ip17, im17, ip35, im35 = i1 + i7, i1 - i7, i3 + i5, i3 - i5
    q1 = C3 * ip17 + C1 * ip35
    q2 = C2 * (im17 + im35)
    q3 = C1 * ip17 - C3 * ip35
    q4 = im17 - im35
    o = [
        sums[0],
        sums[1] - q1,
        sums[2] - q2,
        sums[3] - q3,
        -q4,
        -sums[3] - q3,
        -sums[2] - q2,
        -sums[1] - q1,
    ]
    return [e[a] + o[a] for a in range(8)] + [e[a] - o[a] for a in range(8)]


def forward_kernel(f, fh, fm, fl, ss, s2, edges, resp, nyq, wave, out_edge, xp, xl):
    step = 16

    def radix(t, carry):
        rows = pl.ds(pl.multiple_of(t * step, step), step)
        far_rows = pl.ds(pl.multiple_of(128 + t * step, step), step)
        parts = radix_forward([f[a, rows, :] for a in range(16)])
        for slot in range(SLOTS):
            for where, value in ((rows, parts[slot][0]), (far_rows, parts[slot][1])):
                high, mid, low = split3(value)
                xp[slot, where, 0:128] = high
                xp[slot, where, 128:256] = mid
                xl[slot, where, :] = low
        return carry

    lax.fori_loop(0, 128 // step, radix, 0)

    def solve(s, carry):
        both = xp[s]
        wide = dot(fh[s], both) + dot(fm[s], both)
        spec = wide[:, 0:128] + wide[:, 128:256]
        spec += dot(fh[s], xl[s]) + dot(fl[s], both[:, 0:128])
        high, mid, low = split3(spec)
        wide = dot(jnp.concatenate([high, mid], axis=1), ss[...])
        bent = wide[:, 0:128] + wide[:, 128:256]
        bent += dot(jnp.concatenate([high, low], axis=1), s2[...])
        wave[s] = bent
        high, mid, low = split3(bent * resp[s])
        many = jnp.concatenate([high, mid, high, mid, low, high], axis=1)
        ends = lax.dot_general(
            edges[...], many, (((1,), (1,)), ((), ())), preferred_element_type=F32
        )
        total = ends[2:3] + (ends[0:1] - ends[1:2]) * nyq[s]
        piece = jnp.concatenate([ends[0:2], total, total], axis=0)
        for e in range(GX):
            out_edge[e, s] = piece
        return carry

    lax.fori_loop(0, SLOTS, solve, 0)


def backward_kernel(me, wave, ends, link0, link1, resp, ranks, back1, back2, ih, im, ind, grad, hs):
    row = lax.broadcasted_iota(jnp.int32, (4, 256), 0)

    def solve(s, carry):
        total = jnp.zeros((4, 256), F32)
        alternate = jnp.zeros((1, 256), F32)
        for e in range(GX):
            n = (me[0] - e + GX) % GX
            piece = ends[e, s]
            total += link0[n, s] * piece[0:1] + link1[n, s] * piece[1:2]
            alternate += piece[2:3]
        total = jnp.where(row == 2, alternate * (1.0 / NX), total)
        high, mid = split2(total)
        left = jnp.concatenate([high, mid, high, jnp.zeros_like(high)], axis=0)
        wide = lax.dot_general(left, ranks[...], (((0,), (0,)), ((), ())), preferred_element_type=F32)
        bent = resp[s] * (wave[s] - wide[:, 0:128]) - wide[:, 128:256]
        high, mid = split2(bent)
        line = dot(jnp.concatenate([high, mid], axis=1), back1[...]) + dot(high, back2[...])
        line = jnp.concatenate([line[:, 0:128], line[:, 128:256] + wide[:, 256:384]], axis=1)
        high, mid = split2(line)
        hs[s] = dot(ih[s], high) + dot(ih[s], mid) + dot(im[s], high)
        return carry

    lax.fori_loop(0, SLOTS, solve, 0)
    step = 8

    def radix(t, carry):
        rows = pl.ds(pl.multiple_of(t * step, step), step)
        far_rows = pl.ds(pl.multiple_of(128 + t * step, step), step)
        for part in range(2):
            lanes = slice(128 * part, 128 * part + 128)
            values = radix_inverse([(hs[s, rows, lanes], hs[s, far_rows, lanes]) for s in range(SLOTS)])
            for a in range(16):
                where = pl.ds(pl.multiple_of(a * 128 + t * step, step), step)
                if part == 0:
                    ind[where, :] = values[a]
                else:
                    grad[0, where, :] = values[a]
        return carry

    lax.fori_loop(0, 128 // step, radix, 0)
    grad[1, 0 : NY - 1, :] = ind[1:NY, :] - ind[0 : NY - 1, :]
    grad[1, NY - 1 : NY, :] = ind[0:1, :] - ind[NY - 1 : NY, :]


def vmem():
    return pl.BlockSpec(memory_space=pltpu.VMEM)


def smem():
    return pl.BlockSpec(memory_space=pltpu.SMEM)


def params():
    return pltpu.CompilerParams(vmem_limit_bytes=56 * 1024 * 1024)


def pack(owner, brick, fill, normals, fractions, offsets):
    return pl.pallas_call(
        pack_kernel,
        out_shape=jax.ShapeDtypeStruct((DEV, 5, 4, 128), F32),
        in_specs=[smem()] * 3 + [vmem()] * 3,
        out_specs=vmem(),
        scratch_shapes=[pltpu.SMEM((DEV,), jnp.int32)],
        compiler_params=params(),
        interpret=INTERPRET,
        name="pack",
    )(owner, brick, fill, normals, fractions, offsets)


def splat(first, recv):
    return pl.pallas_call(
        splat_kernel,
        out_shape=jax.ShapeDtypeStruct((Z, NY // GY, 128), F32),
        in_specs=[smem(), vmem()],
        out_specs=vmem(),
        scratch_shapes=[pltpu.VMEM((32, 192, 128), F32)],
        compiler_params=params(),
        interpret=INTERPRET,
        name="splat",
    )(first, recv)


def forward(f):
    t = tables()
    return pl.pallas_call(
        forward_kernel,
        out_shape=(
            jax.ShapeDtypeStruct((SLOTS, 256, 128), F32),
            jax.ShapeDtypeStruct((GX, SLOTS, 4, 256), F32),
        ),
        in_specs=[vmem()] * 9,
        out_specs=(vmem(), vmem()),
        scratch_shapes=[pltpu.VMEM((SLOTS, 256, 256), BF16), pltpu.VMEM((SLOTS, 256, 128), BF16)],
        compiler_params=params(),
        interpret=INTERPRET,
        name="forward",
    )(f, t["fh"], t["fm"], t["fl"], t["ss"], t["s2"], t["edges"], t["resp"], t["nyq"])


def backward(me, wave, ends):
    t = tables()
    return pl.pallas_call(
        backward_kernel,
        out_shape=(
            jax.ShapeDtypeStruct((NY, 128), F32),
            jax.ShapeDtypeStruct((2, NY, 128), F32),
        ),
        in_specs=[smem()] + [vmem()] * 10,
        out_specs=(vmem(), vmem()),
        scratch_shapes=[pltpu.VMEM((SLOTS, 256, 256), F32)],
        compiler_params=params(),
        interpret=INTERPRET,
        name="backward",
    )(
        me, wave, ends, t["link0"], t["link1"], t["resp"], t["ranks"], t["back1"], t["back2"],
        t["ih"], t["im"],
    )


def shards(normals, fractions, offsets, owner, brick, fill):
    send = pack(owner[:, 0], brick, fill, normals, fractions, offsets)
    recv = lax.all_to_all(send, ("gx", "gy"), split_axis=0, concat_axis=0, tiled=True)
    first = recv[:, 4, 0::2, 0].astype(jnp.int32).reshape(2 * DEV)
    tile = splat(first, recv)
    plane = lax.all_to_all(tile, "gy", split_axis=0, concat_axis=0, tiled=True)
    wave, edge = forward(plane.reshape(16, 128, 128))
    ends = lax.all_to_all(edge, "gx", split_axis=0, concat_axis=0, tiled=True)
    me = lax.axis_index("gx").astype(jnp.int32).reshape(1)
    ind, grad = backward(me, wave, ends)
    return ind[None], grad[:, None]


def solution(mesh):
    in_specs = (
        P(("gx", "gy"), None, None),
        P(("gx", "gy"), None, None),
        P(("gx", "gy"), None),
        P(("gx", "gy"), None),
        P(("gx", "gy")),
        P(("gx", "gy")),
    )
    out_specs = (P("gy", None, "gx"), P(None, "gy", None, "gx"))
    return jax.shard_map(shards, mesh=mesh, in_specs=in_specs, out_specs=out_specs, check_vma=False)
```

time: 369 us -> 143 us (0.39)
  matrix products: 121 us -> 0 us
  waiting for transfers between devices: 95.5 us -> 11.4 us
  other arithmetic: 72.9 us -> 2.23 us
  Pallas kernels: 0 us -> 67.2 us
  blocking collectives: 0 us -> 53.3 us
  starting transfers between devices: 41.9 us -> 3.57 us
  local copies, waits for them, and re-layouts: 31.6 us -> 4.07 us
    dot_general x44 -> x0, matrix products: 121 us -> none  [the longest x36 78.7 us: contract(): jnp.einsum(letters + ',' + letters[position] + 'z->' + target, values, ma...]
    all_to_all x7 -> x1, waiting for transfers between devices: 93.3 us -> 11.4 us  [shards(): ends = lax.all_to_all(edge, 'gx', split_axis=0, concat_axis=0, tiled=True)]
    pallas_call x0 -> x4, Pallas kernels: none -> 67.2 us  [the longest x1 43.1 us: splat(): pl.pallas_call(splat_kernel, out_shape=jax.ShapeDtypeStruct((Z, NY // GY,...]
    all_to_all x0 -> x2, blocking collectives: none -> 53.3 us  [the longest x1 33.1 us: shards(): lax.all_to_all(send, ('gx', 'gy'), split_axis=0, concat_axis=0, tiled=True)]
    sub x17 -> x0, other arithmetic: 37.5 us -> none  [the longest x8 35.9 us: splat_blocks(): lower_col - upper_col]
    all_to_all x7 -> x1, starting transfers between devices: 40.4 us -> 3.57 us  [shards(): ends = lax.all_to_all(edge, 'gx', split_axis=0, concat_axis=0, tiled=True)]
    scatter-add x8 -> x0, other arithmetic: 17.1 us -> none  [accumulate(): return (totals.at[pieces[1][:, 0]].add(brick_tiles), None)]
    scatter x2 -> x0, local copies, waits for them, and re-layouts: 14.6 us -> none  [the longest x1 13.7 us: shards(): jnp.zeros((total_slots, 5, points), jnp.float32).at[slot_ids].set(payload)]
  transfers between devices with their start and end apart: 8 -> 1, of which waited for: 7 -> 1; matrix products, arithmetic and copies ran while one was open for 10% -> 0% of each run, Pallas kernels for 0% -> 0%
where the time goes in v1:
time: 143 us; the launch traced here: 142 us
  Pallas kernels  67.2 us (47%)
  blocking collectives  53.3 us (37%)
  waiting for transfers between devices  11.4 us (8%)
  local copies, waits for them, and re-layouts  4.07 us (3%)
  starting transfers between devices  3.57 us (2%)
  other arithmetic  2.23 us (2%)
    pallas_call x1, Pallas kernels, splat(): pl.pallas_call(splat_kernel, out_shape=jax.ShapeDtypeStruct((Z, NY // GY,...  43.1 us
    all_to_all x1, blocking collectives, shards(): lax.all_to_all(send, ('gx', 'gy'), split_axis=0, concat_axis=0, tiled=True)  33.1 us
    all_to_all x1, blocking collectives, shards(): plane = lax.all_to_all(tile, 'gy', split_axis=0, concat_axis=0, tiled=True)  20.2 us
    all_to_all x1, waiting for transfers between devices, shards(): ends = lax.all_to_all(edge, 'gx', split_axis=0, concat_axis=0, tiled=True)  11.4 us
    pallas_call x1, Pallas kernels, backward(): pl.pallas_call(backward_kernel, out_shape=(jax.ShapeDtypeStruct((NY, 128)...  11.3 us
    pallas_call x1, Pallas kernels, forward(): pl.pallas_call(forward_kernel, out_shape=(jax.ShapeDtypeStruct((SLOTS, 25...  9.64 us
    all_to_all x1, starting transfers between devices, shards(): ends = lax.all_to_all(edge, 'gx', split_axis=0, concat_axis=0, tiled=True)  3.57 us
    pallas_call x1, Pallas kernels, pack(): pl.pallas_call(pack_kernel, out_shape=jax.ShapeDtypeStruct((DEV, 5, 4, 12...  3.22 us
  transfers between devices with their start and end apart: 1, of which 1 were waited for; matrix products, arithmetic and copies ran while one was open for 0% of the time, Pallas kernels for 0%

profile of v1, /device:TPU:0, one launch (start us, length us, event | category | flops | bytes accessed | tf_op | source)
XLA Modules:
  0.0 142.4 jit_solution(15525697422728425724)
XLA Ops:
  0.6 3.2 %pack.1 = f32[128,5,4,128]{3,2,1,0:T(4,128)} custom-call(s32[128]{0:T(128)} %bitcast.8, s32[128]{0:T(128)} %brick.1, s32[128]{0:T(128)} %fill.1, f32[128,2,256]{2,1,0:T(2,128)} %normals.1, f32[128,2,256]{2,1,0:T(2,128)} %fractions.1, s32[128,256]{1,0:T(8,128)} %offsets.1), custom_call_target="tpu_custom_call" | custom-call | tf_op jit(solution)/shard_map/pack/pallas_call | solution.py:403
  3.9 33.1 %all_to_all.15.recv = f32[128,5,4,128]{3,2,1,0:T(4,128)S(1)} all-to-all(f32[128,5,4,128]{3,2,1,0:T(4,128)} %pack.1), channel_id=1, replica_groups=mesh['gx'=16,'gy'=8] {'gx','gy'}, dimensions={0} | all-to-all | bytes 2621440 | tf_op jit(solution)/shard_map/all_to_all | solution.py:467
  36.9 0.0 copy-start
  36.9 2.6 %slice.3 = f32[128,1,2,1]{3,2,1,0:T(2,128)S(1)} slice(f32[128,5,4,128]{3,2,1,0:T(4,128)S(1)} %all_to_all.15.recv), slice={[0:128:1], [4:5:1], [0:4:2], [0:1:1]} | slice | bytes 2048 | tf_op jit(solution)/shard_map/slice | solution.py:468
  39.5 2.2 %convert_reduce_fusion = s32[128,2]{1,0:T(8,128)S(1)} fusion(f32[128,1,2,1]{3,2,1,0:T(2,128)S(1)} %slice.3), kind=kLoop, calls=%fused_computation | loop fusion | flops 256 | bytes 2048 | tf_op jit(solution)/shard_map/convert_element_type | solution.py:468
  41.7 0.7 convert_element_type.8.first
  42.4 0.0 copy-done
  42.4 43.1 %splat.1 = f32[8,256,128]{2,1,0:T(8,128)} custom-call(s32[256]{0:T(256)} %convert_element_type.8.first, f32[128,5,4,128]{3,2,1,0:T(4,128)} %copy-done), custom_call_target="tpu_custom_call" | custom-call | tf_op jit(solution)/shard_map/splat/pallas_call | solution.py:416
  85.5 20.2 %all_to_all.16 = f32[8,256,128]{2,1,0:T(8,128)} all-to-all(f32[8,256,128]{2,1,0:T(8,128)} %splat.1), channel_id=1, replica_groups=mesh['gx'=16,'gy'=8] {'gy'}, dimensions={0} | all-to-all | bytes 2097152 | tf_op jit(solution)/shard_map/all_to_all | solution.py:470
  105.7 9.6 %forward.1 = (f32[8,256,128]{2,1,0:T(8,128)}, f32[16,8,4,256]{3,2,1,0:T(4,128)}) custom-call(f32[16,128,128]{2,1,0:T(8,128)} %bitcast.7, bf16[8,256,256]{2,1,0:T(8,128)(2,1)} %constant.36.clone.fh, bf16[8,256,256]{2,1,0:T(8,128)(2,1)} %constant.37.clone.fm, bf16[8,256,256]{2,1,0:T(8,128)(2,1)} %constant.38.clone.fl, bf16[256,256]{1,0:T(8,128)(2,1)} %constant.39.clone.ss, ...), custom_call_target="tpu_custom_call" | custom-call | tf_op jit(solution)/shard_map/forward/pallas_call | solution.py:430
  115.3 3.6 %all-to-all-start.2 = ((f32[16,8,4,256]{3,2,1,0:T(4,128)}), f32[16,8,4,256]{3,2,1,0:T(4,128)S(1)}, u32[]{:S(2)}, u32[]{:S(2)}) async-start(f32[16,8,4,256]{3,2,1,0:T(4,128)} %get-tuple-element.7), calls=%async_computation.2 | async-start | bytes 1048576 | tf_op jit(solution)/shard_map/all_to_all | solution.py:472
  118.9 11.4 %all-to-all-done.2.ends = f32[16,8,4,256]{3,2,1,0:T(4,128)S(1)} async-done(((f32[16,8,4,256]{3,2,1,0:T(4,128)}), f32[16,8,4,256]{3,2,1,0:T(4,128)S(1)}, u32[]{:S(2)}, u32[]{:S(2)}) %all-to-all-start.2) | async-done | bytes 524320 | tf_op jit(solution)/shard_map/all_to_all | solution.py:472
  130.3 0.0 copy-start.1
  130.3 0.8 copy-done.1
  131.1 11.3 %backward.1 = (f32[2048,128]{1,0:T(8,128)}, f32[2,2048,128]{2,1,0:T(8,128)}) custom-call(s32[1]{0:T(128)} %bitcast.me, f32[8,256,128]{2,1,0:T(8,128)} %get-tuple-element.6.wave, f32[16,8,4,256]{3,2,1,0:T(4,128)} %copy-done.1, f32[16,8,4,256]{3,2,1,0:T(4,128)} %constant.44.clone.link0, f32[16,8,4,256]{3,2,1,0:T(4,128)} %constant.45.clone.link1, ...), custom_call_target="tpu_custom_call" | custom-call | tf_op jit(solution)/shard_map/backward/pallas_call | solution.py:447
Async XLA Ops:
  36.9 5.5 %copy-start = (f32[128,5,4,128]{3,2,1,0:T(4,128)}, f32[128,5,4,128]{3,2,1,0:T(4,128)S(1)}, u32[]{:S(2)}) copy-start(f32[128,5,4,128]{3,2,1,0:T(4,128)S(1)} %all_to_all.15.recv) | copy-start | bytes 3932164
  115.3 15.0 %all-to-all-start.2 = ((f32[16,8,4,256]{3,2,1,0:T(4,128)}), f32[16,8,4,256]{3,2,1,0:T(4,128)S(1)}, u32[]{:S(2)}, u32[]{:S(2)}) async-start(f32[16,8,4,256]{3,2,1,0:T(4,128)} %get-tuple-element.7), calls=%async_computation.2 | async-start | bytes 1048576 | tf_op jit(solution)/shard_map/all_to_all | solution.py:472
  130.3 0.8 copy-start.1

commit v2 on v1

--- a/solution.py
+++ b/solution.py
@@ -26,6 +26,9 @@
 C2 = math.cos(math.pi / 4)
 C3 = math.cos(3 * math.pi / 8)
 INTERPRET = False
+SPLAT_UNROLL = 16
+SLOT_UNROLL = 8
+RADIX_UNROLL = 2
 
 
 def np_split(values, parts):
@@ -165,7 +168,7 @@
     lax.fori_loop(0, blocks, one, 0, unroll=4)
 
 
-def splat_kernel(first, recv, out, acc):
+def splat_kernel(recv, out, acc):
     bricks = acc.shape[0]
 
     def clear(l, carry):
@@ -173,69 +176,74 @@
         return carry
 
     lax.fori_loop(0, bricks, clear, 0)
-    rows = lax.broadcasted_iota(jnp.int32, (64, 128), 0)
-    cols = lax.broadcasted_iota(jnp.int32, (128, 128), 0)
-
-    def spread(row, matrix):
-        return jnp.broadcast_to(row, matrix.shape)
-
-    def one_slot(d, slot):
+    rows = lax.broadcasted_iota(jnp.int32, (32, 128), 0).astype(F32).astype(BF16)
+    cols = lax.broadcasted_iota(jnp.int32, (256, 128), 0).astype(F32).astype(BF16)
+    zero = jnp.zeros((), BF16)
+    one_b = jnp.ones((), BF16)
+
+    def spread(row, count):
+        tile = jnp.broadcast_to(row, (16, 128)).astype(BF16)
+        return jnp.concatenate([tile] * (count // 16), axis=0)
+
+    def build(d, slot):
         cell2 = recv[d, 4][2 * slot : 2 * slot + 2].astype(jnp.int32)
-        norm = recv[d, 2 * slot]
-        frac = recv[d, 2 * slot + 1]
-        filled = first[2 * d + slot] >= 0
-        norm = jnp.where(filled, norm, 0.0)
-        frac = jnp.where(filled, frac, 0.0)
+        filled = cell2[0:1] >= 0
+        norm = jnp.where(filled, recv[d, 2 * slot], 0.0)
+        frac = jnp.where(filled, recv[d, 2 * slot + 1], 0.0)
         far = norm * frac
         near = norm * (1.0 - frac)
         near_h = near.astype(BF16).astype(F32)
         far_h = far.astype(BF16).astype(F32)
         near_l = near - near_h
         far_l = far - far_h
-        line2 = (cell2 >> 7) & 63
-        col2 = cell2 & 127
-        high, low, right = [], [], []
+        line2 = (((cell2 >> 11) & 3) * 8 + ((cell2 >> 7) & 7)).astype(F32)
+        next2 = line2 + 1.0
+        col2 = (((cell2 >> 10) & 1) * 128 + (cell2 & 127)).astype(F32)
+        left, right = [], []
         for half in range(2):
-            line = spread(line2[half : half + 1], rows)
-            here = line == rows
-            below = line + 1 == rows
+            here = spread(line2[half : half + 1], 32) == rows
+            below = spread(next2[half : half + 1], 32) == rows
             x = 2 * half
-            for parts, near_v, far_v in ((high, near_h, far_h), (low, near_l, far_l)):
-                flux_x = jnp.where(
-                    here,
-                    spread(near_v[x : x + 1], rows),
-                    jnp.where(below, spread(far_v[x : x + 1], rows), 0.0),
-                )
-                flux_y0 = jnp.where(here, spread(near_v[x + 1 : x + 2], rows), 0.0)
-                flux_y1 = jnp.where(here, spread(far_v[x + 1 : x + 2], rows), 0.0)
+            parts = []
+            for near_v, far_v in ((near_h, far_h), (near_l, far_l)):
                 parts.append(
-                    jnp.concatenate(
-                        [flux_x.astype(BF16), flux_y0.astype(BF16), flux_y1.astype(BF16)], axis=0
+                    jnp.where(
+                        here,
+                        spread(near_v[x : x + 1], 32),
+                        jnp.where(below, spread(far_v[x : x + 1], 32), zero),
                     )
                 )
-            right.append((spread(col2[half : half + 1], cols) == cols).astype(F32).astype(BF16))
-        left = jnp.concatenate(high, axis=1)
-        left_low = jnp.concatenate(low, axis=1)
-        right = jnp.concatenate(right, axis=1)
-        dims = (((1,), (1,)), ((), ()))
-        piece = lax.dot_general(left, right, dims, preferred_element_type=F32)
-        return piece + lax.dot_general(left_low, right, dims, preferred_element_type=F32)
-
-    def one(d, carry):
-        pieces = [one_slot(d, 0), one_slot(d, 1)]
-        for slot in range(2):
-            l = jnp.maximum(first[2 * d + slot], 0) >> 13
-            acc[l] += pieces[slot]
-        return carry
-
-    lax.fori_loop(0, DEV, one, 0)
+                parts.append(jnp.where(here, spread(near_v[x + 1 : x + 2], 32), zero))
+                parts.append(jnp.where(here, spread(far_v[x + 1 : x + 2], 32), zero))
+            left.append(jnp.concatenate(parts, axis=0))
+            right.append(jnp.where(spread(col2[half : half + 1], 256) == cols, one_b, zero))
+        piece = lax.dot_general(
+            jnp.concatenate(left, axis=1),
+            jnp.concatenate(right, axis=1),
+            (((1,), (1,)), ((), ())),
+            preferred_element_type=F32,
+        )
+        return piece[0:96] + piece[96:192], jnp.maximum(cell2[0, 0] >> 13, 0)
+
+    group = 2 * SPLAT_UNROLL
+
+    def one(i, carry):
+        for piece, l in [build(i * SPLAT_UNROLL + k // 2, k % 2) for k in range(group)]:
+            acc[l] += piece
+        return carry
+
+    lax.fori_loop(0, DEV // SPLAT_UNROLL, one, 0)
 
     def finish(l, carry):
-        flux_x = acc[l, 0:64].reshape(Z, BY, 128)
-        flux_y = (acc[l, 64:128] + pltpu.roll(acc[l, 128:192], 1, axis=1)).reshape(Z, BY, 128)
-        moved_x = pltpu.roll(acc[l, 0:64], 1, axis=1).reshape(Z, BY, 128)
-        tile = flux_x - moved_x + flux_y - pltpu.roll(flux_y, 1, axis=1)
-        out[:, pl.ds(pl.multiple_of(l * BY, BY), BY), :] = tile
+        for odd in range(2):
+            lanes = slice(128 * odd, 128 * odd + 128)
+            flux_x = acc[l, 0:32, lanes]
+            flux_y = acc[l, 32:64, lanes] + pltpu.roll(acc[l, 64:96, lanes], 1, axis=1)
+            moved_x = pltpu.roll(flux_x, 1, axis=1)
+            flux_y = flux_y.reshape(4, BY, 128)
+            tile = (flux_x - moved_x).reshape(4, BY, 128) + flux_y - pltpu.roll(flux_y, 1, axis=1)
+            for plane in range(4):
+                out[2 * plane + odd, pl.ds(pl.multiple_of(l * BY, BY), BY), :] = tile[plane]
         return carry
 
     lax.fori_loop(0, bricks, finish, 0)
@@ -316,7 +324,7 @@
                 xl[slot, where, :] = low
         return carry
 
-    lax.fori_loop(0, 128 // step, radix, 0)
+    lax.fori_loop(0, 128 // step, radix, 0, unroll=RADIX_UNROLL)
 
     def solve(s, carry):
         both = xp[s]
@@ -339,7 +347,7 @@
             out_edge[e, s] = piece
         return carry
 
-    lax.fori_loop(0, SLOTS, solve, 0)
+    lax.fori_loop(0, SLOTS, solve, 0, unroll=SLOT_UNROLL)
 
 
 def backward_kernel(me, wave, ends, link0, link1, resp, ranks, back1, back2, ih, im, ind, grad, hs):
@@ -365,7 +373,7 @@
         hs[s] = dot(ih[s], high) + dot(ih[s], mid) + dot(im[s], high)
         return carry
 
-    lax.fori_loop(0, SLOTS, solve, 0)
+    lax.fori_loop(0, SLOTS, solve, 0, unroll=SLOT_UNROLL)
     step = 8
 
     def radix(t, carry):
@@ -382,7 +390,7 @@
                     grad[0, where, :] = values[a]
         return carry
 
-    lax.fori_loop(0, 128 // step, radix, 0)
+    lax.fori_loop(0, 128 // step, radix, 0, unroll=RADIX_UNROLL)
     grad[1, 0 : NY - 1, :] = ind[1:NY, :] - ind[0 : NY - 1, :]
     grad[1, NY - 1 : NY, :] = ind[0:1, :] - ind[NY - 1 : NY, :]
 
@@ -395,8 +403,8 @@
     return pl.BlockSpec(memory_space=pltpu.SMEM)
 
 
-def params():
-    return pltpu.CompilerParams(vmem_limit_bytes=56 * 1024 * 1024)
+def params(mib):
+    return pltpu.CompilerParams(vmem_limit_bytes=mib * 1024 * 1024)
 
 
 def pack(owner, brick, fill, normals, fractions, offsets):
@@ -406,23 +414,23 @@
         in_specs=[smem()] * 3 + [vmem()] * 3,
         out_specs=vmem(),
         scratch_shapes=[pltpu.SMEM((DEV,), jnp.int32)],
-        compiler_params=params(),
+        compiler_params=params(6),
         interpret=INTERPRET,
         name="pack",
     )(owner, brick, fill, normals, fractions, offsets)
 
 
-def splat(first, recv):
+def splat(recv):
     return pl.pallas_call(
         splat_kernel,
         out_shape=jax.ShapeDtypeStruct((Z, NY // GY, 128), F32),
-        in_specs=[smem(), vmem()],
+        in_specs=[vmem()],
         out_specs=vmem(),
-        scratch_shapes=[pltpu.VMEM((32, 192, 128), F32)],
-        compiler_params=params(),
+        scratch_shapes=[pltpu.VMEM((32, 96, 256), F32)],
+        compiler_params=params(12),
         interpret=INTERPRET,
         name="splat",
-    )(first, recv)
+    )(recv)
 
 
 def forward(f):
@@ -436,7 +444,7 @@
         in_specs=[vmem()] * 9,
         out_specs=(vmem(), vmem()),
         scratch_shapes=[pltpu.VMEM((SLOTS, 256, 256), BF16), pltpu.VMEM((SLOTS, 256, 128), BF16)],
-        compiler_params=params(),
+        compiler_params=params(16),
         interpret=INTERPRET,
         name="forward",
     )(f, t["fh"], t["fm"], t["fl"], t["ss"], t["s2"], t["edges"], t["resp"], t["nyq"])
@@ -453,7 +461,7 @@
         in_specs=[smem()] + [vmem()] * 10,
         out_specs=(vmem(), vmem()),
         scratch_shapes=[pltpu.VMEM((SLOTS, 256, 256), F32)],
-        compiler_params=params(),
+        compiler_params=params(16),
         interpret=INTERPRET,
         name="backward",
     )(
@@ -465,8 +473,7 @@
 def shards(normals, fractions, offsets, owner, brick, fill):
     send = pack(owner[:, 0], brick, fill, normals, fractions, offsets)
     recv = lax.all_to_all(send, ("gx", "gy"), split_axis=0, concat_axis=0, tiled=True)
-    first = recv[:, 4, 0::2, 0].astype(jnp.int32).reshape(2 * DEV)
-    tile = splat(first, recv)
+    tile = splat(recv)
     plane = lax.all_to_all(tile, "gy", split_axis=0, concat_axis=0, tiled=True)
     wave, edge = forward(plane.reshape(16, 128, 128))
     ends = lax.all_to_all(edge, "gx", split_axis=0, concat_axis=0, tiled=True)

time: 143 us -> 106 us (0.74)
  Pallas kernels: 67.2 us -> 28.8 us
  local copies, waits for them, and re-layouts: 4.07 us -> 9.29 us
  other arithmetic: 2.23 us -> 0 us
  blocking collectives: 53.3 us -> 51.4 us
    pallas_call x1, Pallas kernels: 43.1 us -> 15.5 us  [splat(): pl.pallas_call(splat_kernel, out_shape=jax.ShapeDtypeStruct((Z, NY // GY,...]
    unnamed x4 -> x46, local copies, waits for them, and re-layouts: 0.81 us -> 9.29 us
    pallas_call x1, Pallas kernels: 11.3 us -> 6.2 us  [backward(): pl.pallas_call(backward_kernel, out_shape=(jax.ShapeDtypeStruct((NY, 128)...]
    pallas_call x1, Pallas kernels: 9.64 us -> 5.46 us  [forward(): pl.pallas_call(forward_kernel, out_shape=(jax.ShapeDtypeStruct((SLOTS, 25...]
    slice x1 -> x0, local copies, waits for them, and re-layouts: 2.56 us -> none  [shards(): first = recv[:, 4, 0::2, 0].astype(jnp.int32).reshape(2 * DEV)]
    convert_element_type x1 -> x0, other arithmetic: 2.23 us -> none  [shards(): first = recv[:, 4, 0::2, 0].astype(jnp.int32).reshape(2 * DEV)]
    all_to_all x1, blocking collectives: 20.2 us -> 18.5 us  [shards(): plane = lax.all_to_all(tile, 'gy', split_axis=0, concat_axis=0, tiled=True)]
    pallas_call x1, Pallas kernels: 3.22 us -> 1.64 us  [pack(): pl.pallas_call(pack_kernel, out_shape=jax.ShapeDtypeStruct((DEV, 5, 4, 12...]
where the time goes in v2:
time: 106 us; the launch traced here: 105 us
  blocking collectives  51.4 us (48%)
  Pallas kernels  28.8 us (27%)
  waiting for transfers between devices  11.4 us (11%)
  local copies, waits for them, and re-layouts  9.29 us (9%)
  starting transfers between devices  3.71 us (4%)
    all_to_all x1, blocking collectives, shards(): lax.all_to_all(send, ('gx', 'gy'), split_axis=0, concat_axis=0, tiled=True)  32.9 us
    all_to_all x1, blocking collectives, shards(): plane = lax.all_to_all(tile, 'gy', split_axis=0, concat_axis=0, tiled=True)  18.5 us
    pallas_call x1, Pallas kernels, splat(): pl.pallas_call(splat_kernel, out_shape=jax.ShapeDtypeStruct((Z, NY // GY,...  15.5 us
    all_to_all x1, waiting for transfers between devices, shards(): ends = lax.all_to_all(edge, 'gx', split_axis=0, concat_axis=0, tiled=True)  11.4 us
    unnamed x46, local copies, waits for them, and re-layouts  9.29 us
    pallas_call x1, Pallas kernels, backward(): pl.pallas_call(backward_kernel, out_shape=(jax.ShapeDtypeStruct((NY, 128)...  6.2 us
    pallas_call x1, Pallas kernels, forward(): pl.pallas_call(forward_kernel, out_shape=(jax.ShapeDtypeStruct((SLOTS, 25...  5.46 us
    all_to_all x1, starting transfers between devices, shards(): ends = lax.all_to_all(edge, 'gx', split_axis=0, concat_axis=0, tiled=True)  3.71 us
  transfers between devices with their start and end apart: 1, of which 1 were waited for; matrix products, arithmetic and copies ran while one was open for 0% of the time, Pallas kernels for 0%

profile of v2, /device:TPU:0, one launch (start us, length us, event | category | flops | bytes accessed | tf_op | source)
XLA Modules:
  0.0 105.4 jit_solution(12767139555443105575)
XLA Ops:
  0.6 0.0 copy-start.10
  0.6 0.9 copy-done.10
  1.6 0.9 copy-done.11
  2.5 0.9 copy-done.12
  3.4 0.7 copy-done.20
  4.1 0.7 copy-done.21
  4.8 0.7 copy-done.22
  5.4 1.6 %pack.1 = f32[128,5,4,128]{3,2,1,0:T(4,128)S(1)} custom-call(s32[128]{0:T(128)S(1)} %bitcast.8, s32[128]{0:T(128)S(1)} %copy-done.21, s32[128]{0:T(128)S(1)} %copy-done.22, f32[128,2,256]{2,1,0:T(2,128)S(1)} %copy-done.10, f32[128,2,256]{2,1,0:T(2,128)S(1)} %copy-done.11, s32[128,256]{1,0:T(8,128)S(1)} %copy-done.12), custom_call_target="tpu_custom_call" | custom-call | tf_op jit(solution)/shard_map/pack/pallas_call | solution.py:411
  7.1 32.9 %all_to_all.15.recv = f32[128,5,4,128]{3,2,1,0:T(4,128)S(1)} all-to-all(f32[128,5,4,128]{3,2,1,0:T(4,128)S(1)} %pack.1), channel_id=1, replica_groups=mesh['gx'=16,'gy'=8] {'gx','gy'}, dimensions={0} | all-to-all | bytes 2621440 | tf_op jit(solution)/shard_map/all_to_all | solution.py:475
  39.9 0.0 copy-start.17
  40.0 0.0 copy-start.19
  40.0 15.5 %splat.1 = f32[8,256,128]{2,1,0:T(8,128)S(1)} custom-call(f32[128,5,4,128]{3,2,1,0:T(4,128)S(1)} %all_to_all.15.recv), custom_call_target="tpu_custom_call" | custom-call | tf_op jit(solution)/shard_map/splat/pallas_call | solution.py:424
  55.5 0.0 copy-start
  55.5 0.0 copy-start.5
  55.5 18.5 %all_to_all.16 = f32[8,256,128]{2,1,0:T(8,128)S(1)} all-to-all(f32[8,256,128]{2,1,0:T(8,128)S(1)} %splat.1), channel_id=1, replica_groups=mesh['gx'=16,'gy'=8] {'gy'}, dimensions={0} | all-to-all | bytes 2097152 | tf_op jit(solution)/shard_map/all_to_all | solution.py:477
  74.0 0.0 copy-done.6
  74.0 0.0 copy-done.7
  74.0 0.0 copy-done.14
  74.1 0.0 copy-start.8
  74.1 0.0 copy-start.13
  74.1 0.0 copy-start.15
  74.1 0.0 copy-start.18
  74.1 5.5 %forward.1 = (f32[8,256,128]{2,1,0:T(8,128)S(1)}, f32[16,8,4,256]{3,2,1,0:T(4,128)}) custom-call(f32[16,128,128]{2,1,0:T(8,128)S(1)} %bitcast.7, bf16[8,256,256]{2,1,0:T(8,128)(2,1)S(1)} %copy-done.7, bf16[8,256,256]{2,1,0:T(8,128)(2,1)S(1)} %copy-done.6, bf16[8,256,256]{2,1,0:T(8,128)(2,1)S(1)} %copy-done.5, bf16[256,256]{1,0:T(8,128)(2,1)S(1)} %copy-done.14, ...), custom_call_target="tpu_custom_call" | custom-call | tf_op jit(solution)/shard_map/forward/pallas_call | solution.py:438
  79.6 1.0 copy-done.3
  80.6 3.7 %all-to-all-start.2 = ((f32[16,8,4,256]{3,2,1,0:T(4,128)}), f32[16,8,4,256]{3,2,1,0:T(4,128)S(1)}, u32[]{:S(2)}, u32[]{:S(2)}) async-start(f32[16,8,4,256]{3,2,1,0:T(4,128)} %get-tuple-element.7), calls=%async_computation.2 | async-start | bytes 1048576 | tf_op jit(solution)/shard_map/all_to_all | solution.py:479
  84.3 11.4 %all-to-all-done.2.ends = f32[16,8,4,256]{3,2,1,0:T(4,128)S(1)} async-done(((f32[16,8,4,256]{3,2,1,0:T(4,128)}), f32[16,8,4,256]{3,2,1,0:T(4,128)S(1)}, u32[]{:S(2)}, u32[]{:S(2)}) %all-to-all-start.2) | async-done | bytes 524320 | tf_op jit(solution)/shard_map/all_to_all | solution.py:479
  95.7 0.0 copy-done.13
  95.7 0.0 copy-start.2
  95.7 1.2 %copy-done.2 = bf16[8,256,256]{2,1,0:T(8,128)(2,1)S(1)} copy-done((bf16[8,256,256]{2,1,0:T(8,128)(2,1)S(1)}, bf16[8,256,256]{2,1,0:T(8,128)(2,1)}, u32[]{:S(2)}) %copy-start.2) | copy-done | bytes 1048600
  97.0 1.2 %copy-done.4 = f32[8,256,128]{2,1,0:T(8,128)S(1)} copy-done((f32[8,256,128]{2,1,0:T(8,128)S(1)}, f32[8,256,128]{2,1,0:T(8,128)}, u32[]{:S(2)}) %copy-start.4) | copy-done | bytes 1048600
  98.2 1.0 copy-done.9
  99.2 6.2 %backward.1 = (f32[2048,128]{1,0:T(8,128)}, f32[2,2048,128]{2,1,0:T(8,128)}) custom-call(s32[1]{0:T(128)} %bitcast.me, f32[8,256,128]{2,1,0:T(8,128)S(1)} %copy-done.4, f32[16,8,4,256]{3,2,1,0:T(4,128)S(1)} %all-to-all-done.2.ends, f32[16,8,4,256]{3,2,1,0:T(4,128)S(1)} %copy-done.9, f32[16,8,4,256]{3,2,1,0:T(4,128)S(1)} %copy-done.8, ...), custom_call_target="tpu_custom_call" | custom-call | tf_op jit(solution)/shard_map/backward/pallas_call | solution.py:455
  (22 shorter events, 0.0 us)
Async XLA Ops:
  0.6 1.0 copy-start.10
  1.6 0.9 copy-start.11
  2.5 0.9 copy-start.12
  3.4 0.7 copy-start.20
  4.1 0.7 copy-start.21
  4.7 0.7 copy-start.22
  39.9 34.1 %copy-start.6 = (bf16[8,256,256]{2,1,0:T(8,128)(2,1)S(1)}, bf16[8,256,256]{2,1,0:T(8,128)(2,1)}, u32[]{:S(2)}) copy-start(bf16[8,256,256]{2,1,0:T(8,128)(2,1)} %constant.37.clone.fm) | copy-start | bytes 3145732
  39.9 34.1 %copy-start.7 = (bf16[8,256,256]{2,1,0:T(8,128)(2,1)S(1)}, bf16[8,256,256]{2,1,0:T(8,128)(2,1)}, u32[]{:S(2)}) copy-start(bf16[8,256,256]{2,1,0:T(8,128)(2,1)} %constant.36.clone.fh) | copy-start | bytes 3145732
  39.9 34.1 %copy-start.14 = (bf16[256,256]{1,0:T(8,128)(2,1)S(1)}, bf16[256,256]{1,0:T(8,128)(2,1)}, u32[]{:S(2)}) copy-start(bf16[256,256]{1,0:T(8,128)(2,1)} %constant.39.clone.ss) | copy-start | bytes 393220
  39.9 34.1 %copy-start.16 = (bf16[256,128]{1,0:T(8,128)(2,1)S(1)}, bf16[256,128]{1,0:T(8,128)(2,1)}, u32[]{:S(2)}) copy-start(bf16[256,128]{1,0:T(8,128)(2,1)} %constant.40.clone.s2) | copy-start | bytes 196612
  39.9 34.1 %copy-start.17 = (bf16[8,768]{1,0:T(8,128)(2,1)S(1)}, bf16[8,768]{1,0:T(8,128)(2,1)}, u32[]{:S(2)}) copy-start(bf16[8,768]{1,0:T(8,128)(2,1)} %constant.41.clone.edges) | copy-start | bytes 36868
  40.0 34.1 %copy-start.19 = (f32[8,1,256]{2,1,0:T(1,128)S(1)}, f32[8,1,256]{2,1,0:T(1,128)}, u32[]{:S(2)}) copy-start(f32[8,1,256]{2,1,0:T(1,128)} %constant.43.clone.nyq) | copy-start | bytes 24580
  55.5 18.6 %copy-start = (f32[8,256,128]{2,1,0:T(8,128)S(1)}, f32[8,256,128]{2,1,0:T(8,128)}, u32[]{:S(2)}) copy-start(f32[8,256,128]{2,1,0:T(8,128)} %constant.42.clone.resp) | copy-start | bytes 3145732
  55.5 18.6 %copy-start.5 = (bf16[8,256,256]{2,1,0:T(8,128)(2,1)S(1)}, bf16[8,256,256]{2,1,0:T(8,128)(2,1)}, u32[]{:S(2)}) copy-start(bf16[8,256,256]{2,1,0:T(8,128)(2,1)} %constant.38.clone.fl) | copy-start | bytes 3145732
  74.1 21.6 %copy-start.8 = (f32[16,8,4,256]{3,2,1,0:T(4,128)S(1)}, f32[16,8,4,256]{3,2,1,0:T(4,128)}, u32[]{:S(2)}) copy-start(f32[16,8,4,256]{3,2,1,0:T(4,128)} %constant.45.clone.link1) | copy-start | bytes 1572868
  74.1 21.6 %copy-start.13 = (bf16[256,256]{1,0:T(8,128)(2,1)S(1)}, bf16[256,256]{1,0:T(8,128)(2,1)}, u32[]{:S(2)}) copy-start(bf16[256,256]{1,0:T(8,128)(2,1)} %constant.47.clone.back1) | copy-start | bytes 393220
  74.1 21.6 %copy-start.15 = (bf16[128,256]{1,0:T(8,128)(2,1)S(1)}, bf16[128,256]{1,0:T(8,128)(2,1)}, u32[]{:S(2)}) copy-start(bf16[128,256]{1,0:T(8,128)(2,1)} %constant.48.clone.back2) | copy-start | bytes 196612
  74.1 21.6 %copy-start.18 = (bf16[16,384]{1,0:T(8,128)(2,1)S(1)}, bf16[16,384]{1,0:T(8,128)(2,1)}, u32[]{:S(2)}) copy-start(bf16[16,384]{1,0:T(8,128)(2,1)} %constant.46.clone.ranks) | copy-start | bytes 36868
  79.6 1.0 copy-start.3
  80.6 15.1 %copy-start.1 = (bf16[8,256,256]{2,1,0:T(8,128)(2,1)S(1)}, bf16[8,256,256]{2,1,0:T(8,128)(2,1)}, u32[]{:S(2)}) copy-start(bf16[8,256,256]{2,1,0:T(8,128)(2,1)} %constant.50.clone.im) | copy-start | bytes 3145732
  80.6 15.1 %all-to-all-start.2 = ((f32[16,8,4,256]{3,2,1,0:T(4,128)}), f32[16,8,4,256]{3,2,1,0:T(4,128)S(1)}, u32[]{:S(2)}, u32[]{:S(2)}) async-start(f32[16,8,4,256]{3,2,1,0:T(4,128)} %get-tuple-element.7), calls=%async_computation.2 | async-start | bytes 1048576 | tf_op jit(solution)/shard_map/all_to_all | solution.py:479
  95.7 1.2 %copy-start.2 = (bf16[8,256,256]{2,1,0:T(8,128)(2,1)S(1)}, bf16[8,256,256]{2,1,0:T(8,128)(2,1)}, u32[]{:S(2)}) copy-start(bf16[8,256,256]{2,1,0:T(8,128)(2,1)} %constant.49.clone.ih) | copy-start | bytes 3145732
  97.0 1.2 %copy-start.4 = (f32[8,256,128]{2,1,0:T(8,128)S(1)}, f32[8,256,128]{2,1,0:T(8,128)}, u32[]{:S(2)}) copy-start(f32[8,256,128]{2,1,0:T(8,128)} %copy-done.3) | copy-start | bytes 3145732
  98.2 1.0 copy-start.9

commit v3 on v2

--- a/solution.py
+++ b/solution.py
@@ -27,8 +27,9 @@
 C3 = math.cos(3 * math.pi / 8)
 INTERPRET = False
 SPLAT_UNROLL = 16
-SLOT_UNROLL = 8
 RADIX_UNROLL = 2
+LF = 24
+LB = 50
 
 
 def np_split(values, parts):
@@ -88,37 +89,33 @@
         n = n % NX
         return -(np.exp(logr * n) + np.exp(logr * (NX - n))) / (root * (1 - np.exp(logr * NX)))
 
-    link0 = np.zeros((GX, SLOTS, 4, 256))
-    link1 = np.zeros((GX, SLOTS, 4, 256))
+    link = np.zeros((2, GX, SLOTS, 256))
     for n in range(GX):
-        link0[n, :, 0] = -green(128 * n)
-        link1[n, :, 0] = -green(128 * (n - 1) - 1) + (1.0 if n == 1 else 0.0)
-        link0[n, :, 1] = -green(128 * (n + 1) + 1) + (1.0 if n == GX - 1 else 0.0)
-        link1[n, :, 1] = -green(128 * n)
+        link[0, n] = -green(128 * n)
+        link[1, n] = -green(128 * (n + 1) + 1) + (1.0 if n == GX - 1 else 0.0)
     fh, fm, fl = np_split(fwd, 3)
     ih, im = np_split(inv, 2)
     sh, sm, sl = np_split(sine, 3)
     ss = np.block([[sh, sm], [sh, sm]])
     s2 = np.concatenate([sl, sh], axis=0)
-    eh, em, el = np_split(edge, 3)
-    edges = np.concatenate([eh, eh, em, em, eh, el], axis=1)
-    diff = np.concatenate([sine[:, 1:], np.zeros((128, 1))], axis=1) - sine
+    eh, em = np_split(edge, 2)
+    edges = np.block([[eh, eh], [em, em]])
     back = np.concatenate([sine.T, np.concatenate([sine.T[:, 1:], np.zeros((128, 1))], axis=1) - sine.T], axis=1)
     bh, bm = np_split(back, 2)
     back1 = np.concatenate([bh, bh], axis=0)
-    rank = np.zeros((4, 384))
+    rank = np.zeros((3, 384))
     rank[0, 0:128] = sine[0]
     rank[1, 0:128] = sine[127]
     rank[2, 128:256] = alt
     rank[1, 256 + 127] = 1.0
     rank[2, 256 + 127] = -1.0
     rh, rm = np_split(rank, 2)
-    ranks = np.concatenate([rh, rh, rm, np.zeros((4, 384), BF16)], axis=0)
+    ranks = np.concatenate([rh, rh, rm, np.zeros((7, 384), BF16)], axis=0)
     f = np.float32
     return dict(
-        fh=fh, fm=fm, fl=fl, ih=ih, im=im, ss=ss, s2=s2, edges=edges, resp=resp.astype(f),
-        nyq=nyq.reshape(SLOTS, 1, 256).astype(f), link0=link0.astype(f), link1=link1.astype(f),
-        back1=back1, back2=bm, ranks=ranks,
+        fwd=np.concatenate([fh, fm, fl], axis=1), inv=np.concatenate([ih, im], axis=1), ss=ss, s2=s2,
+        edges=edges, resp=resp.astype(f), nyq=nyq.reshape(SLOTS, 1, 256).astype(f),
+        link=link.astype(f), back1=back1, back2=bm, ranks=ranks,
     )
 
 
@@ -309,7 +306,7 @@
     return [e[a] + o[a] for a in range(8)] + [e[a] - o[a] for a in range(8)]
 
 
-def forward_kernel(f, fh, fm, fl, ss, s2, edges, resp, nyq, wave, out_edge, xp, xl):
+def forward_kernel(f, fwd, ss, s2, edges, resp, nyq, wave, out_edge, xh, xm, xl, ends_all):
     step = 16
 
     def radix(t, carry):
@@ -318,62 +315,71 @@
         parts = radix_forward([f[a, rows, :] for a in range(16)])
         for slot in range(SLOTS):
             for where, value in ((rows, parts[slot][0]), (far_rows, parts[slot][1])):
-                high, mid, low = split3(value)
-                xp[slot, where, 0:128] = high
-                xp[slot, where, 128:256] = mid
-                xl[slot, where, :] = low
+                xh[slot, where, :], xm[slot, where, :], xl[slot, where, :] = split3(value)
         return carry
 
     lax.fori_loop(0, 128 // step, radix, 0, unroll=RADIX_UNROLL)
-
-    def solve(s, carry):
-        both = xp[s]
-        wide = dot(fh[s], both) + dot(fm[s], both)
-        spec = wide[:, 0:128] + wide[:, 128:256]
-        spec += dot(fh[s], xl[s]) + dot(fl[s], both[:, 0:128])
+    for s in range(SLOTS):
+        wide = dot(fwd[s], jnp.concatenate([xh[s], xm[s]], axis=1))
+        spec = dot(fwd[s, 0:256], xl[s]) + wide[512:768, 0:128]
+        spec += wide[256:512, 0:128] + wide[0:256, 128:256] + wide[256:512, 128:256]
+        spec += wide[0:256, 0:128]
         high, mid, low = split3(spec)
         wide = dot(jnp.concatenate([high, mid], axis=1), ss[...])
-        bent = wide[:, 0:128] + wide[:, 128:256]
-        bent += dot(jnp.concatenate([high, low], axis=1), s2[...])
+        bent = dot(jnp.concatenate([high, low], axis=1), s2[...])
+        bent += wide[:, 128:256] + wide[:, 0:128]
         wave[s] = bent
-        high, mid, low = split3(bent * resp[s])
-        many = jnp.concatenate([high, mid, high, mid, low, high], axis=1)
+        high, mid = split2(bent * resp[s])
         ends = lax.dot_general(
-            edges[...], many, (((1,), (1,)), ((), ())), preferred_element_type=F32
+            edges[...],
+            jnp.concatenate([high, mid], axis=1),
+            (((1,), (1,)), ((), ())),
+            preferred_element_type=F32,
         )
-        total = ends[2:3] + (ends[0:1] - ends[1:2]) * nyq[s]
-        piece = jnp.concatenate([ends[0:2], total, total], axis=0)
-        for e in range(GX):
-            out_edge[e, s] = piece
-        return carry
-
-    lax.fori_loop(0, SLOTS, solve, 0, unroll=SLOT_UNROLL)
-
-
-def backward_kernel(me, wave, ends, link0, link1, resp, ranks, back1, back2, ih, im, ind, grad, hs):
-    row = lax.broadcasted_iota(jnp.int32, (4, 256), 0)
-
-    def solve(s, carry):
-        total = jnp.zeros((4, 256), F32)
-        alternate = jnp.zeros((1, 256), F32)
-        for e in range(GX):
-            n = (me[0] - e + GX) % GX
-            piece = ends[e, s]
-            total += link0[n, s] * piece[0:1] + link1[n, s] * piece[1:2]
-            alternate += piece[2:3]
-        total = jnp.where(row == 2, alternate * (1.0 / NX), total)
-        high, mid = split2(total)
-        left = jnp.concatenate([high, mid, high, jnp.zeros_like(high)], axis=0)
-        wide = lax.dot_general(left, ranks[...], (((0,), (0,)), ((), ())), preferred_element_type=F32)
+        ends = ends[0:8] + ends[8:16]
+        ends_all[0, s : s + 1] = ends[0:1]
+        ends_all[1, s : s + 1] = ends[1:2]
+        ends_all[2, s : s + 1] = ends[2:3] + (ends[0:1] - ends[1:2]) * nyq[s]
+    for e in range(GX):
+        out_edge[e] = ends_all[...]
+
+
+def backward_kernel(me, wave, ends, link, resp, ranks, back1, back2, inv, ind, grad, hs, invs, sems):
+    copies = []
+    for s in range(SLOTS):
+        copy = pltpu.make_async_copy(inv.at[s], invs.at[s], sems.at[s])
+        copy.start()
+        copies.append(copy)
+    left = jnp.zeros((SLOTS, 256), F32)
+    right = jnp.zeros((SLOTS, 256), F32)
+    swing = jnp.zeros((SLOTS, 256), F32)
+    for e in range(GX):
+        n = (me[0] - e + GX) % GX
+        first, last = ends[e, 0], ends[e, 1]
+        near = link[0, n]
+        left += near * first + link[1, (GX - n) % GX] * last
+        right += link[1, n] * first + near * last
+        swing += ends[e, 2]
+    swing *= 1.0 / NX
+    values = []
+    for value in (left, right, swing):
+        high = value.astype(BF16).astype(F32)
+        values.append((high, value - high))
+    for s in range(SLOTS):
+        highs = [high[s : s + 1] for high, _ in values]
+        mids = [mid[s : s + 1] for _, mid in values]
+        stack = jnp.concatenate(highs + mids + highs + [jnp.zeros((7, 256), F32)], axis=0)
+        wide = lax.dot_general(
+            stack.astype(BF16), ranks[...], (((0,), (0,)), ((), ())), preferred_element_type=F32
+        )
         bent = resp[s] * (wave[s] - wide[:, 0:128]) - wide[:, 128:256]
         high, mid = split2(bent)
         line = dot(jnp.concatenate([high, mid], axis=1), back1[...]) + dot(high, back2[...])
         line = jnp.concatenate([line[:, 0:128], line[:, 128:256] + wide[:, 256:384]], axis=1)
         high, mid = split2(line)
-        hs[s] = dot(ih[s], high) + dot(ih[s], mid) + dot(im[s], high)
-        return carry
-
-    lax.fori_loop(0, SLOTS, solve, 0, unroll=SLOT_UNROLL)
+        copies[s].wait()
+        wide = dot(invs[s], high)
+        hs[s] = dot(invs[s, 0:256], mid) + wide[256:512] + wide[0:256]
     step = 8
 
     def radix(t, carry):
@@ -414,7 +420,7 @@
         in_specs=[smem()] * 3 + [vmem()] * 3,
         out_specs=vmem(),
         scratch_shapes=[pltpu.SMEM((DEV,), jnp.int32)],
-        compiler_params=params(6),
+        compiler_params=params(56),
         interpret=INTERPRET,
         name="pack",
     )(owner, brick, fill, normals, fractions, offsets)
@@ -433,21 +439,26 @@
     )(recv)
 
 
+def hbm():
+    return pl.BlockSpec(memory_space=pltpu.HBM)
+
+
 def forward(f):
     t = tables()
     return pl.pallas_call(
         forward_kernel,
         out_shape=(
             jax.ShapeDtypeStruct((SLOTS, 256, 128), F32),
-            jax.ShapeDtypeStruct((GX, SLOTS, 4, 256), F32),
+            jax.ShapeDtypeStruct((GX, 3, SLOTS, 256), F32),
         ),
-        in_specs=[vmem()] * 9,
+        in_specs=[vmem()] * 7,
         out_specs=(vmem(), vmem()),
-        scratch_shapes=[pltpu.VMEM((SLOTS, 256, 256), BF16), pltpu.VMEM((SLOTS, 256, 128), BF16)],
-        compiler_params=params(16),
+        scratch_shapes=[pltpu.VMEM((SLOTS, 256, 128), BF16)] * 3
+        + [pltpu.VMEM((3, SLOTS, 256), F32)],
+        compiler_params=params(LF),
         interpret=INTERPRET,
         name="forward",
-    )(f, t["fh"], t["fm"], t["fl"], t["ss"], t["s2"], t["edges"], t["resp"], t["nyq"])
+    )(f, t["fwd"], t["ss"], t["s2"], t["edges"], t["resp"], t["nyq"])
 
 
 def backward(me, wave, ends):
@@ -458,16 +469,17 @@
             jax.ShapeDtypeStruct((NY, 128), F32),
             jax.ShapeDtypeStruct((2, NY, 128), F32),
         ),
-        in_specs=[smem()] + [vmem()] * 10,
+        in_specs=[smem()] + [vmem()] * 7 + [hbm()],
         out_specs=(vmem(), vmem()),
-        scratch_shapes=[pltpu.VMEM((SLOTS, 256, 256), F32)],
-        compiler_params=params(16),
+        scratch_shapes=[
+            pltpu.VMEM((SLOTS, 256, 256), F32),
+            pltpu.VMEM((SLOTS, 512, 256), BF16),
+            pltpu.SemaphoreType.DMA((SLOTS,)),
+        ],
+        compiler_params=params(LB),
         interpret=INTERPRET,
         name="backward",
-    )(
-        me, wave, ends, t["link0"], t["link1"], t["resp"], t["ranks"], t["back1"], t["back2"],
-        t["ih"], t["im"],
-    )
+    )(me, wave, ends, t["link"], t["resp"], t["ranks"], t["back1"], t["back2"], t["inv"])
 
 
 def shards(normals, fractions, offsets, owner, brick, fill):

time: 106 us -> 96.7 us (0.912)
  local copies, waits for them, and re-layouts: 9.29 us -> 0.06 us
  Pallas kernels: 28.8 us -> 30.6 us
  waiting for transfers between devices: 11.4 us -> 9.96 us
    unnamed x46 -> x20, local copies, waits for them, and re-layouts: 9.29 us -> 0.06 us
    pallas_call x1, Pallas kernels: 1.64 us -> 3.22 us  [pack(): pl.pallas_call(pack_kernel, out_shape=jax.ShapeDtypeStruct((DEV, 5, 4, 12...]
    all_to_all x1, waiting for transfers between devices: 11.4 us -> 9.96 us  [shards(): ends = lax.all_to_all(edge, 'gx', split_axis=0, concat_axis=0, tiled=True)]
where the time goes in v3:
time: 96.7 us; the launch traced here: 96.4 us
  blocking collectives  51.5 us (53%)
  Pallas kernels  30.6 us (32%)
  waiting for transfers between devices  9.96 us (10%)
  starting transfers between devices  3.55 us (4%)
    all_to_all x1, blocking collectives, shards(): lax.all_to_all(send, ('gx', 'gy'), split_axis=0, concat_axis=0, tiled=True)  33.1 us
    all_to_all x1, blocking collectives, shards(): plane = lax.all_to_all(tile, 'gy', split_axis=0, concat_axis=0, tiled=True)  18.4 us
    pallas_call x1, Pallas kernels, splat(): pl.pallas_call(splat_kernel, out_shape=jax.ShapeDtypeStruct((Z, NY // GY,...  15.5 us
    all_to_all x1, waiting for transfers between devices, shards(): ends = lax.all_to_all(edge, 'gx', split_axis=0, concat_axis=0, tiled=True)  9.96 us
    pallas_call x1, Pallas kernels, backward(): pl.pallas_call(backward_kernel, out_shape=(jax.ShapeDtypeStruct((NY, 128)...  7.12 us
    pallas_call x1, Pallas kernels, forward(): pl.pallas_call(forward_kernel, out_shape=(jax.ShapeDtypeStruct((SLOTS, 25...  4.74 us
    all_to_all x1, starting transfers between devices, shards(): ends = lax.all_to_all(edge, 'gx', split_axis=0, concat_axis=0, tiled=True)  3.55 us
    pallas_call x1, Pallas kernels, pack(): pl.pallas_call(pack_kernel, out_shape=jax.ShapeDtypeStruct((DEV, 5, 4, 12...  3.22 us
  transfers between devices with their start and end apart: 1, of which 1 were waited for; matrix products, arithmetic and copies ran while one was open for 0% of the time, Pallas kernels for 0%

profile of v3, /device:TPU:0, one launch (start us, length us, event | category | flops | bytes accessed | tf_op | source)
XLA Modules:
  0.0 96.4 jit_solution(3912063660000882266)
XLA Ops:
  0.6 3.2 %pack.1 = f32[128,5,4,128]{3,2,1,0:T(4,128)} custom-call(s32[128]{0:T(128)} %bitcast.8, s32[128]{0:T(128)} %brick.1, s32[128]{0:T(128)} %fill.1, f32[128,2,256]{2,1,0:T(2,128)} %normals.1, f32[128,2,256]{2,1,0:T(2,128)} %fractions.1, s32[128,256]{1,0:T(8,128)} %offsets.1), custom_call_target="tpu_custom_call" | custom-call | tf_op jit(solution)/shard_map/pack/pallas_call | solution.py:417
  3.9 33.1 %all_to_all.15.recv = f32[128,5,4,128]{3,2,1,0:T(4,128)S(1)} all-to-all(f32[128,5,4,128]{3,2,1,0:T(4,128)} %pack.1), channel_id=1, replica_groups=mesh['gx'=16,'gy'=8] {'gx','gy'}, dimensions={0} | all-to-all | bytes 2621440 | tf_op jit(solution)/shard_map/all_to_all | solution.py:487
  36.9 0.0 copy-start
  36.9 0.0 copy-start.1
  36.9 0.0 copy-start.4
  36.9 0.0 copy-start.6
  36.9 0.0 copy-start.8
  37.0 0.0 copy-start.9
  37.0 15.5 %splat.1 = f32[8,256,128]{2,1,0:T(8,128)S(1)} custom-call(f32[128,5,4,128]{3,2,1,0:T(4,128)S(1)} %all_to_all.15.recv), custom_call_target="tpu_custom_call" | custom-call | tf_op jit(solution)/shard_map/splat/pallas_call | solution.py:430
  52.5 18.4 %all_to_all.16 = f32[8,256,128]{2,1,0:T(8,128)S(1)} all-to-all(f32[8,256,128]{2,1,0:T(8,128)S(1)} %splat.1), channel_id=1, replica_groups=mesh['gx'=16,'gy'=8] {'gy'}, dimensions={0} | all-to-all | bytes 2097152 | tf_op jit(solution)/shard_map/all_to_all | solution.py:489
  70.9 0.0 copy-done
  70.9 0.0 copy-done.1
  70.9 0.0 copy-done.4
  70.9 0.0 copy-done.6
  70.9 0.0 copy-done.8
  70.9 0.0 copy-done.9
  70.9 0.0 copy-start.2
  70.9 0.0 copy-start.3
  70.9 0.0 copy-start.5
  70.9 0.0 copy-start.7
  71.0 4.7 %forward.1 = (f32[8,256,128]{2,1,0:T(8,128)S(1)}, f32[16,3,8,256]{3,2,1,0:T(8,128)}) custom-call(f32[16,128,128]{2,1,0:T(8,128)S(1)} %bitcast.7, bf16[8,768,256]{2,1,0:T(8,128)(2,1)S(1)} %copy-done.1, bf16[256,256]{1,0:T(8,128)(2,1)S(1)} %copy-done.4, bf16[256,128]{1,0:T(8,128)(2,1)S(1)} %copy-done.6, bf16[16,256]{1,0:T(8,128)(2,1)S(1)} %copy-done.9, ...), custom_call_target="tpu_custom_call" | custom-call | tf_op jit(solution)/shard_map/forward/pallas_call | solution.py:448
  75.7 3.6 %all-to-all-start.2 = ((f32[16,3,8,256]{3,2,1,0:T(8,128)}), f32[16,3,8,256]{3,2,1,0:T(8,128)S(1)}, u32[]{:S(2)}, u32[]{:S(2)}) async-start(f32[16,3,8,256]{3,2,1,0:T(8,128)} %get-tuple-element.7), calls=%async_computation.2 | async-start | bytes 786432 | tf_op jit(solution)/shard_map/all_to_all | solution.py:491
  79.3 10.0 %all-to-all-done.2.ends = f32[16,3,8,256]{3,2,1,0:T(8,128)S(1)} async-done(((f32[16,3,8,256]{3,2,1,0:T(8,128)}), f32[16,3,8,256]{3,2,1,0:T(8,128)S(1)}, u32[]{:S(2)}, u32[]{:S(2)}) %all-to-all-start.2) | async-done | bytes 393248 | tf_op jit(solution)/shard_map/all_to_all | solution.py:491
  89.2 0.0 copy-done.2
  89.2 0.0 copy-done.3
  89.2 0.0 copy-done.5
  89.2 0.0 copy-done.7
  89.2 7.1 %backward.1 = (f32[2048,128]{1,0:T(8,128)}, f32[2,2048,128]{2,1,0:T(8,128)}) custom-call(s32[1]{0:T(128)} %bitcast.me, f32[8,256,128]{2,1,0:T(8,128)S(1)} %get-tuple-element.6.wave, f32[16,3,8,256]{3,2,1,0:T(8,128)S(1)} %all-to-all-done.2.ends, f32[2,16,8,256]{3,2,1,0:T(8,128)S(1)} %copy-done.2, f32[8,256,128]{2,1,0:T(8,128)S(1)} %copy-done, ...), custom_call_target="tpu_custom_call" | custom-call | tf_op jit(solution)/shard_map/backward/pallas_call | solution.py:466
Async XLA Ops:
  36.9 33.9 %copy-start = (f32[8,256,128]{2,1,0:T(8,128)S(1)}, f32[8,256,128]{2,1,0:T(8,128)}, u32[]{:S(2)}) copy-start(f32[8,256,128]{2,1,0:T(8,128)} %constant.32.clone.resp) | copy-start | bytes 3145732
  36.9 33.9 %copy-start.1 = (bf16[8,768,256]{2,1,0:T(8,128)(2,1)S(1)}, bf16[8,768,256]{2,1,0:T(8,128)(2,1)}, u32[]{:S(2)}) copy-start(bf16[8,768,256]{2,1,0:T(8,128)(2,1)} %constant.28.clone.fwd) | copy-start | bytes 9437188
  36.9 33.9 %copy-start.4 = (bf16[256,256]{1,0:T(8,128)(2,1)S(1)}, bf16[256,256]{1,0:T(8,128)(2,1)}, u32[]{:S(2)}) copy-start(bf16[256,256]{1,0:T(8,128)(2,1)} %constant.29.clone.ss) | copy-start | bytes 393220
  36.9 33.9 %copy-start.6 = (bf16[256,128]{1,0:T(8,128)(2,1)S(1)}, bf16[256,128]{1,0:T(8,128)(2,1)}, u32[]{:S(2)}) copy-start(bf16[256,128]{1,0:T(8,128)(2,1)} %constant.30.clone.s2) | copy-start | bytes 196612
  36.9 33.9 %copy-start.8 = (f32[8,1,256]{2,1,0:T(1,128)S(1)}, f32[8,1,256]{2,1,0:T(1,128)}, u32[]{:S(2)}) copy-start(f32[8,1,256]{2,1,0:T(1,128)} %constant.33.clone.nyq) | copy-start | bytes 24580
  37.0 33.9 %copy-start.9 = (bf16[16,256]{1,0:T(8,128)(2,1)S(1)}, bf16[16,256]{1,0:T(8,128)(2,1)}, u32[]{:S(2)}) copy-start(bf16[16,256]{1,0:T(8,128)(2,1)} %constant.31.clone.edges) | copy-start | bytes 24580
  70.9 18.3 %copy-start.2 = (f32[2,16,8,256]{3,2,1,0:T(8,128)S(1)}, f32[2,16,8,256]{3,2,1,0:T(8,128)}, u32[]{:S(2)}) copy-start(f32[2,16,8,256]{3,2,1,0:T(8,128)} %constant.34.clone.link) | copy-start | bytes 786436
  70.9 18.3 %copy-start.3 = (bf16[256,256]{1,0:T(8,128)(2,1)S(1)}, bf16[256,256]{1,0:T(8,128)(2,1)}, u32[]{:S(2)}) copy-start(bf16[256,256]{1,0:T(8,128)(2,1)} %constant.36.clone.back1) | copy-start | bytes 393220
  70.9 18.3 %copy-start.5 = (bf16[128,256]{1,0:T(8,128)(2,1)S(1)}, bf16[128,256]{1,0:T(8,128)(2,1)}, u32[]{:S(2)}) copy-start(bf16[128,256]{1,0:T(8,128)(2,1)} %constant.37.clone.back2) | copy-start | bytes 196612
  70.9 18.3 %copy-start.7 = (bf16[16,384]{1,0:T(8,128)(2,1)S(1)}, bf16[16,384]{1,0:T(8,128)(2,1)}, u32[]{:S(2)}) copy-start(bf16[16,384]{1,0:T(8,128)(2,1)} %constant.35.clone.ranks) | copy-start | bytes 36868
  75.7 13.5 %all-to-all-start.2 = ((f32[16,3,8,256]{3,2,1,0:T(8,128)}), f32[16,3,8,256]{3,2,1,0:T(8,128)S(1)}, u32[]{:S(2)}, u32[]{:S(2)}) async-start(f32[16,3,8,256]{3,2,1,0:T(8,128)} %get-tuple-element.7), calls=%async_computation.2 | async-start | bytes 786432 | tf_op jit(solution)/shard_map/all_to_all | solution.py:491

commit v4 on v3

--- a/solution.py
+++ b/solution.py
@@ -26,10 +26,14 @@
 C2 = math.cos(math.pi / 4)
 C3 = math.cos(3 * math.pi / 8)
 INTERPRET = False
-SPLAT_UNROLL = 16
+SPLAT_UNROLL = 32
+FINISH_UNROLL = 8
+FGROUP = 8
+BGROUP = 4
 RADIX_UNROLL = 2
+CHUNKS = 4
 LF = 24
-LB = 50
+LB = 51
 
 
 def np_split(values, parts):
@@ -243,7 +247,7 @@
                 out[2 * plane + odd, pl.ds(pl.multiple_of(l * BY, BY), BY), :] = tile[plane]
         return carry
 
-    lax.fori_loop(0, bricks, finish, 0)
+    lax.fori_loop(0, bricks, finish, 0, unroll=FINISH_UNROLL)
 
 
 def radix_forward(f):
@@ -319,16 +323,22 @@
         return carry
 
     lax.fori_loop(0, 128 // step, radix, 0, unroll=RADIX_UNROLL)
-    for s in range(SLOTS):
+
+    def to_frequency(s):
         wide = dot(fwd[s], jnp.concatenate([xh[s], xm[s]], axis=1))
         spec = dot(fwd[s, 0:256], xl[s]) + wide[512:768, 0:128]
         spec += wide[256:512, 0:128] + wide[0:256, 128:256] + wide[256:512, 128:256]
-        spec += wide[0:256, 0:128]
+        return spec + wide[0:256, 0:128]
+
+    def to_sine(s, spec):
         high, mid, low = split3(spec)
         wide = dot(jnp.concatenate([high, mid], axis=1), ss[...])
         bent = dot(jnp.concatenate([high, low], axis=1), s2[...])
         bent += wide[:, 128:256] + wide[:, 0:128]
         wave[s] = bent
+        return bent
+
+    def to_ends(s, bent):
         high, mid = split2(bent * resp[s])
         ends = lax.dot_general(
             edges[...],
@@ -340,11 +350,18 @@
         ends_all[0, s : s + 1] = ends[0:1]
         ends_all[1, s : s + 1] = ends[1:2]
         ends_all[2, s : s + 1] = ends[2:3] + (ends[0:1] - ends[1:2]) * nyq[s]
+
+    for first in range(0, SLOTS, FGROUP):
+        group = range(first, first + FGROUP)
+        specs = [to_frequency(s) for s in group]
+        waves = [to_sine(s, spec) for s, spec in zip(group, specs)]
+        for s, bent in zip(group, waves):
+            to_ends(s, bent)
     for e in range(GX):
         out_edge[e] = ends_all[...]
 
 
-def backward_kernel(me, wave, ends, link, resp, ranks, back1, back2, inv, ind, grad, hs, invs, sems):
+def backward_kernel(me, wave, ends, link, resp, ranks, back1, back2, inv, ind_out, grad_out, hs, invs, sems, parts_all, out_sems):
     copies = []
     for s in range(SLOTS):
         copy = pltpu.make_async_copy(inv.at[s], invs.at[s], sems.at[s])
@@ -365,40 +382,75 @@
     for value in (left, right, swing):
         high = value.astype(BF16).astype(F32)
         values.append((high, value - high))
-    for s in range(SLOTS):
+
+    def couple(s):
         highs = [high[s : s + 1] for high, _ in values]
         mids = [mid[s : s + 1] for _, mid in values]
         stack = jnp.concatenate(highs + mids + highs + [jnp.zeros((7, 256), F32)], axis=0)
-        wide = lax.dot_general(
+        return lax.dot_general(
             stack.astype(BF16), ranks[...], (((0,), (0,)), ((), ())), preferred_element_type=F32
         )
+
+    def to_columns(s, wide):
         bent = resp[s] * (wave[s] - wide[:, 0:128]) - wide[:, 128:256]
         high, mid = split2(bent)
         line = dot(jnp.concatenate([high, mid], axis=1), back1[...]) + dot(high, back2[...])
-        line = jnp.concatenate([line[:, 0:128], line[:, 128:256] + wide[:, 256:384]], axis=1)
+        return jnp.concatenate([line[:, 0:128], line[:, 128:256] + wide[:, 256:384]], axis=1)
+
+    def to_rows(s, line):
         high, mid = split2(line)
         copies[s].wait()
         wide = dot(invs[s], high)
         hs[s] = dot(invs[s, 0:256], mid) + wide[256:512] + wide[0:256]
+
+    for first in range(0, SLOTS, BGROUP):
+        group = range(first, first + BGROUP)
+        wides = [couple(s) for s in group]
+        lines = [to_columns(s, wide) for s, wide in zip(group, wides)]
+        for s, line in zip(group, lines):
+            to_rows(s, line)
     step = 8
-
-    def radix(t, carry):
-        rows = pl.ds(pl.multiple_of(t * step, step), step)
-        far_rows = pl.ds(pl.multiple_of(128 + t * step, step), step)
-        for part in range(2):
-            lanes = slice(128 * part, 128 * part + 128)
-            values = radix_inverse([(hs[s, rows, lanes], hs[s, far_rows, lanes]) for s in range(SLOTS)])
-            for a in range(16):
-                where = pl.ds(pl.multiple_of(a * 128 + t * step, step), step)
-                if part == 0:
-                    ind[where, :] = values[a]
-                else:
-                    grad[0, where, :] = values[a]
-        return carry
-
-    lax.fori_loop(0, 128 // step, radix, 0, unroll=RADIX_UNROLL)
-    grad[1, 0 : NY - 1, :] = ind[1:NY, :] - ind[0 : NY - 1, :]
-    grad[1, NY - 1 : NY, :] = ind[0:1, :] - ind[NY - 1 : NY, :]
+    chunk = 128 // CHUNKS
+    outgoing = []
+
+    def send(part, rows):
+        target = (ind_out, grad_out.at[0], grad_out.at[1])[part]
+        copy = pltpu.make_async_copy(
+            parts_all.at[part, :, rows, :], target.at[:, rows, :], out_sems.at[len(outgoing)]
+        )
+        copy.start()
+        outgoing.append(copy)
+
+    ind, grad_x, grad_y = parts_all.at[0], parts_all.at[1], parts_all.at[2]
+    for c in reversed(range(CHUNKS)):
+
+        def radix(t, carry):
+            start = c * chunk + t * step
+            rows = pl.ds(pl.multiple_of(start, step), step)
+            far_rows = pl.ds(pl.multiple_of(128 + start, step), step)
+            for part in range(2):
+                lanes = slice(128 * part, 128 * part + 128)
+                values = radix_inverse(
+                    [(hs[s, rows, lanes], hs[s, far_rows, lanes]) for s in range(SLOTS)]
+                )
+                for a in range(16):
+                    parts_all[part, a, rows, :] = values[a]
+            return carry
+
+        lax.fori_loop(0, chunk // step, radix, 0, unroll=RADIX_UNROLL)
+        rows = pl.ds(c * chunk, chunk)
+        send(0, rows)
+        send(1, rows)
+        low, high = c * chunk, min((c + 1) * chunk, 127)
+        for a in range(16):
+            grad_y[a, low:high, :] = ind[a, low + 1 : high + 1, :] - ind[a, low:high, :]
+        if c < CHUNKS - 1:
+            send(2, rows)
+    for a in range(16):
+        grad_y[a, 127:128, :] = ind[(a + 1) % 16, 0:1, :] - ind[a, 127:128, :]
+    send(2, pl.ds(128 - chunk, chunk))
+    for copy in outgoing:
+        copy.wait()
 
 
 def vmem():
@@ -466,15 +518,17 @@
     return pl.pallas_call(
         backward_kernel,
         out_shape=(
-            jax.ShapeDtypeStruct((NY, 128), F32),
-            jax.ShapeDtypeStruct((2, NY, 128), F32),
+            jax.ShapeDtypeStruct((16, 128, 128), F32),
+            jax.ShapeDtypeStruct((2, 16, 128, 128), F32),
         ),
         in_specs=[smem()] + [vmem()] * 7 + [hbm()],
-        out_specs=(vmem(), vmem()),
+        out_specs=(hbm(), hbm()),
         scratch_shapes=[
             pltpu.VMEM((SLOTS, 256, 256), F32),
             pltpu.VMEM((SLOTS, 512, 256), BF16),
             pltpu.SemaphoreType.DMA((SLOTS,)),
+            pltpu.VMEM((3, 16, 128, 128), F32),
+            pltpu.SemaphoreType.DMA((3 * CHUNKS,)),
         ],
         compiler_params=params(LB),
         interpret=INTERPRET,
@@ -491,7 +545,7 @@
     ends = lax.all_to_all(edge, "gx", split_axis=0, concat_axis=0, tiled=True)
     me = lax.axis_index("gx").astype(jnp.int32).reshape(1)
     ind, grad = backward(me, wave, ends)
-    return ind[None], grad[:, None]
+    return ind.reshape(1, NY, 128), grad.reshape(2, 1, NY, 128)
 
 
 def solution(mesh):

time: 96.7 us -> 91.5 us (0.946)
  Pallas kernels: 30.6 us -> 25.4 us
    pallas_call x1, Pallas kernels: 15.5 us -> 12.6 us  [splat(): pl.pallas_call(splat_kernel, out_shape=jax.ShapeDtypeStruct((Z, NY // GY,...]
    pallas_call x1, Pallas kernels: 4.74 us -> 3.23 us  [forward(): pl.pallas_call(forward_kernel, out_shape=(jax.ShapeDtypeStruct((SLOTS, 25...]
where the time goes in v4:
time: 91.5 us; the launch traced here: 91.1 us
  blocking collectives  51.5 us (56%)
  Pallas kernels  25.4 us (28%)
  waiting for transfers between devices  9.96 us (11%)
  starting transfers between devices  3.55 us (4%)
    all_to_all x1, blocking collectives, shards(): lax.all_to_all(send, ('gx', 'gy'), split_axis=0, concat_axis=0, tiled=True)  33.1 us
    all_to_all x1, blocking collectives, shards(): plane = lax.all_to_all(tile, 'gy', split_axis=0, concat_axis=0, tiled=True)  18.4 us
    pallas_call x1, Pallas kernels, splat(): pl.pallas_call(splat_kernel, out_shape=jax.ShapeDtypeStruct((Z, NY // GY,...  12.6 us
    all_to_all x1, waiting for transfers between devices, shards(): ends = lax.all_to_all(edge, 'gx', split_axis=0, concat_axis=0, tiled=True)  9.96 us
    pallas_call x1, Pallas kernels, backward(): pl.pallas_call(backward_kernel, out_shape=(jax.ShapeDtypeStruct((16, 128,...  6.31 us
    all_to_all x1, starting transfers between devices, shards(): ends = lax.all_to_all(edge, 'gx', split_axis=0, concat_axis=0, tiled=True)  3.55 us
    pallas_call x1, Pallas kernels, forward(): pl.pallas_call(forward_kernel, out_shape=(jax.ShapeDtypeStruct((SLOTS, 25...  3.23 us
    pallas_call x1, Pallas kernels, pack(): pl.pallas_call(pack_kernel, out_shape=jax.ShapeDtypeStruct((DEV, 5, 4, 12...  3.22 us
  transfers between devices with their start and end apart: 1, of which 1 were waited for; matrix products, arithmetic and copies ran while one was open for 0% of the time, Pallas kernels for 0%

profile of v4, /device:TPU:0, one launch (start us, length us, event | category | flops | bytes accessed | tf_op | source)
XLA Modules:
  0.0 91.1 jit_solution(5986946573901739908)
XLA Ops:
  0.6 3.2 %pack.1 = f32[128,5,4,128]{3,2,1,0:T(4,128)} custom-call(s32[128]{0:T(128)} %bitcast.8, s32[128]{0:T(128)} %brick.1, s32[128]{0:T(128)} %fill.1, f32[128,2,256]{2,1,0:T(2,128)} %normals.1, f32[128,2,256]{2,1,0:T(2,128)} %fractions.1, s32[128,256]{1,0:T(8,128)} %offsets.1), custom_call_target="tpu_custom_call" | custom-call | tf_op jit(solution)/shard_map/pack/pallas_call | solution.py:469
  3.9 33.1 %all_to_all.15.recv = f32[128,5,4,128]{3,2,1,0:T(4,128)S(1)} all-to-all(f32[128,5,4,128]{3,2,1,0:T(4,128)} %pack.1), channel_id=1, replica_groups=mesh['gx'=16,'gy'=8] {'gx','gy'}, dimensions={0} | all-to-all | bytes 2621440 | tf_op jit(solution)/shard_map/all_to_all | solution.py:541
  36.9 0.0 copy-start
  36.9 0.0 copy-start.1
  36.9 0.0 copy-start.4
  36.9 0.0 copy-start.6
  36.9 0.0 copy-start.8
  37.0 0.0 copy-start.9
  37.0 12.6 %splat.1 = f32[8,256,128]{2,1,0:T(8,128)S(1)} custom-call(f32[128,5,4,128]{3,2,1,0:T(4,128)S(1)} %all_to_all.15.recv), custom_call_target="tpu_custom_call" | custom-call | tf_op jit(solution)/shard_map/splat/pallas_call | solution.py:482
  49.6 18.4 %all_to_all.16 = f32[8,256,128]{2,1,0:T(8,128)S(1)} all-to-all(f32[8,256,128]{2,1,0:T(8,128)S(1)} %splat.1), channel_id=1, replica_groups=mesh['gx'=16,'gy'=8] {'gy'}, dimensions={0} | all-to-all | bytes 2097152 | tf_op jit(solution)/shard_map/all_to_all | solution.py:543
  68.0 0.0 copy-done
  68.0 0.0 copy-done.1
  68.0 0.0 copy-done.4
  68.0 0.0 copy-done.6
  68.0 0.0 copy-done.8
  68.0 0.0 copy-done.9
  68.0 0.0 copy-start.2
  68.0 0.0 copy-start.3
  68.0 0.0 copy-start.5
  68.0 0.0 copy-start.7
  68.1 3.2 %forward.1 = (f32[8,256,128]{2,1,0:T(8,128)S(1)}, f32[16,3,8,256]{3,2,1,0:T(8,128)}) custom-call(f32[16,128,128]{2,1,0:T(8,128)S(1)} %bitcast.7, bf16[8,768,256]{2,1,0:T(8,128)(2,1)S(1)} %copy-done.1, bf16[256,256]{1,0:T(8,128)(2,1)S(1)} %copy-done.4, bf16[256,128]{1,0:T(8,128)(2,1)S(1)} %copy-done.6, bf16[16,256]{1,0:T(8,128)(2,1)S(1)} %copy-done.9, ...), custom_call_target="tpu_custom_call" | custom-call | tf_op jit(solution)/shard_map/forward/pallas_call | solution.py:500
  71.3 3.6 %all-to-all-start.2 = ((f32[16,3,8,256]{3,2,1,0:T(8,128)}), f32[16,3,8,256]{3,2,1,0:T(8,128)S(1)}, u32[]{:S(2)}, u32[]{:S(2)}) async-start(f32[16,3,8,256]{3,2,1,0:T(8,128)} %get-tuple-element.7), calls=%async_computation.2 | async-start | bytes 786432 | tf_op jit(solution)/shard_map/all_to_all | solution.py:545
  74.8 10.0 %all-to-all-done.2.ends = f32[16,3,8,256]{3,2,1,0:T(8,128)S(1)} async-done(((f32[16,3,8,256]{3,2,1,0:T(8,128)}), f32[16,3,8,256]{3,2,1,0:T(8,128)S(1)}, u32[]{:S(2)}, u32[]{:S(2)}) %all-to-all-start.2) | async-done | bytes 393248 | tf_op jit(solution)/shard_map/all_to_all | solution.py:545
  84.8 0.0 copy-done.2
  84.8 0.0 copy-done.3
  84.8 0.0 copy-done.5
  84.8 0.0 copy-done.7
  84.8 6.3 %backward.1 = (f32[16,128,128]{2,1,0:T(8,128)}, f32[2,16,128,128]{3,2,1,0:T(8,128)}) custom-call(s32[1]{0:T(128)} %bitcast.me, f32[8,256,128]{2,1,0:T(8,128)S(1)} %get-tuple-element.6.wave, f32[16,3,8,256]{3,2,1,0:T(8,128)S(1)} %all-to-all-done.2.ends, f32[2,16,8,256]{3,2,1,0:T(8,128)S(1)} %copy-done.2, f32[8,256,128]{2,1,0:T(8,128)S(1)} %copy-done, ...), custom_call_target="tpu_custom_call" | custom-call | tf_op jit(solution)/shard_map/backward/pallas_call | solution.py:518
Async XLA Ops:
  36.9 31.0 %copy-start = (f32[8,256,128]{2,1,0:T(8,128)S(1)}, f32[8,256,128]{2,1,0:T(8,128)}, u32[]{:S(2)}) copy-start(f32[8,256,128]{2,1,0:T(8,128)} %constant.32.clone.resp) | copy-start | bytes 3145732
  36.9 31.0 %copy-start.1 = (bf16[8,768,256]{2,1,0:T(8,128)(2,1)S(1)}, bf16[8,768,256]{2,1,0:T(8,128)(2,1)}, u32[]{:S(2)}) copy-start(bf16[8,768,256]{2,1,0:T(8,128)(2,1)} %constant.28.clone.fwd) | copy-start | bytes 9437188
  36.9 31.0 %copy-start.4 = (bf16[256,256]{1,0:T(8,128)(2,1)S(1)}, bf16[256,256]{1,0:T(8,128)(2,1)}, u32[]{:S(2)}) copy-start(bf16[256,256]{1,0:T(8,128)(2,1)} %constant.29.clone.ss) | copy-start | bytes 393220
  36.9 31.0 %copy-start.6 = (bf16[256,128]{1,0:T(8,128)(2,1)S(1)}, bf16[256,128]{1,0:T(8,128)(2,1)}, u32[]{:S(2)}) copy-start(bf16[256,128]{1,0:T(8,128)(2,1)} %constant.30.clone.s2) | copy-start | bytes 196612
  36.9 31.0 %copy-start.8 = (f32[8,1,256]{2,1,0:T(1,128)S(1)}, f32[8,1,256]{2,1,0:T(1,128)}, u32[]{:S(2)}) copy-start(f32[8,1,256]{2,1,0:T(1,128)} %constant.33.clone.nyq) | copy-start | bytes 24580
  37.0 31.0 %copy-start.9 = (bf16[16,256]{1,0:T(8,128)(2,1)S(1)}, bf16[16,256]{1,0:T(8,128)(2,1)}, u32[]{:S(2)}) copy-start(bf16[16,256]{1,0:T(8,128)(2,1)} %constant.31.clone.edges) | copy-start | bytes 24580
  68.0 16.8 %copy-start.2 = (f32[2,16,8,256]{3,2,1,0:T(8,128)S(1)}, f32[2,16,8,256]{3,2,1,0:T(8,128)}, u32[]{:S(2)}) copy-start(f32[2,16,8,256]{3,2,1,0:T(8,128)} %constant.34.clone.link) | copy-start | bytes 786436
  68.0 16.8 %copy-start.3 = (bf16[256,256]{1,0:T(8,128)(2,1)S(1)}, bf16[256,256]{1,0:T(8,128)(2,1)}, u32[]{:S(2)}) copy-start(bf16[256,256]{1,0:T(8,128)(2,1)} %constant.36.clone.back1) | copy-start | bytes 393220
  68.0 16.8 %copy-start.5 = (bf16[128,256]{1,0:T(8,128)(2,1)S(1)}, bf16[128,256]{1,0:T(8,128)(2,1)}, u32[]{:S(2)}) copy-start(bf16[128,256]{1,0:T(8,128)(2,1)} %constant.37.clone.back2) | copy-start | bytes 196612
  68.0 16.8 %copy-start.7 = (bf16[16,384]{1,0:T(8,128)(2,1)S(1)}, bf16[16,384]{1,0:T(8,128)(2,1)}, u32[]{:S(2)}) copy-start(bf16[16,384]{1,0:T(8,128)(2,1)} %constant.35.clone.ranks) | copy-start | bytes 36868
  71.3 13.5 %all-to-all-start.2 = ((f32[16,3,8,256]{3,2,1,0:T(8,128)}), f32[16,3,8,256]{3,2,1,0:T(8,128)S(1)}, u32[]{:S(2)}, u32[]{:S(2)}) async-start(f32[16,3,8,256]{3,2,1,0:T(8,128)} %get-tuple-element.7), calls=%async_computation.2 | async-start | bytes 786432 | tf_op jit(solution)/shard_map/all_to_all | solution.py:545

commit v5 on v4

--- a/solution.py
+++ b/solution.py
@@ -27,13 +27,15 @@
 C3 = math.cos(3 * math.pi / 8)
 INTERPRET = False
 SPLAT_UNROLL = 32
-FINISH_UNROLL = 8
+FINISH_UNROLL = 16
 FGROUP = 8
 BGROUP = 4
 RADIX_UNROLL = 2
 CHUNKS = 4
 LF = 24
 LB = 51
+LP = 56
+PACK_UNROLL = 16
 
 
 def np_split(values, parts):
@@ -166,7 +168,7 @@
         send[d, 4] = jnp.where(row4 // 2 == slot, jnp.concatenate([two, two], axis=0), send[d, 4])
         return carry
 
-    lax.fori_loop(0, blocks, one, 0, unroll=4)
+    lax.fori_loop(0, blocks, one, 0, unroll=PACK_UNROLL)
 
 
 def splat_kernel(recv, out, acc):
@@ -239,10 +241,12 @@
         for odd in range(2):
             lanes = slice(128 * odd, 128 * odd + 128)
             flux_x = acc[l, 0:32, lanes]
-            flux_y = acc[l, 32:64, lanes] + pltpu.roll(acc[l, 64:96, lanes], 1, axis=1)
-            moved_x = pltpu.roll(flux_x, 1, axis=1)
-            flux_y = flux_y.reshape(4, BY, 128)
-            tile = (flux_x - moved_x).reshape(4, BY, 128) + flux_y - pltpu.roll(flux_y, 1, axis=1)
+            near_y = acc[l, 32:64, lanes].reshape(4, BY, 128)
+            far_y = acc[l, 64:96, lanes].reshape(4, BY, 128)
+            near_y = near_y - pltpu.roll(near_y, 1, axis=1)
+            far_y = far_y - pltpu.roll(far_y, 1, axis=1)
+            moved = pltpu.roll(far_y.reshape(32, 128) - flux_x, 1, axis=1)
+            tile = (flux_x + near_y.reshape(32, 128) + moved).reshape(4, BY, 128)
             for plane in range(4):
                 out[2 * plane + odd, pl.ds(pl.multiple_of(l * BY, BY), BY), :] = tile[plane]
         return carry
@@ -462,7 +466,7 @@
 
 
 def params(mib):
-    return pltpu.CompilerParams(vmem_limit_bytes=mib * 1024 * 1024)
+    return pltpu.CompilerParams(vmem_limit_bytes=int(mib * 1024 * 1024))
 
 
 def pack(owner, brick, fill, normals, fractions, offsets):
@@ -472,7 +476,7 @@
         in_specs=[smem()] * 3 + [vmem()] * 3,
         out_specs=vmem(),
         scratch_shapes=[pltpu.SMEM((DEV,), jnp.int32)],
-        compiler_params=params(56),
+        compiler_params=params(LP),
         interpret=INTERPRET,
         name="pack",
     )(owner, brick, fill, normals, fractions, offsets)

time: 91.5 us -> 90.9 us (level)
  no operation moved by 1% of the time
where the time goes in v5:
time: 90.9 us; the launch traced here: 90.6 us
  blocking collectives  51.5 us (57%)
  Pallas kernels  24.8 us (27%)
  waiting for transfers between devices  9.96 us (11%)
  starting transfers between devices  3.55 us (4%)
    all_to_all x1, blocking collectives, shards(): lax.all_to_all(send, ('gx', 'gy'), split_axis=0, concat_axis=0, tiled=True)  33.1 us
    all_to_all x1, blocking collectives, shards(): plane = lax.all_to_all(tile, 'gy', split_axis=0, concat_axis=0, tiled=True)  18.4 us
    pallas_call x1, Pallas kernels, splat(): pl.pallas_call(splat_kernel, out_shape=jax.ShapeDtypeStruct((Z, NY // GY,...  12.2 us
    all_to_all x1, waiting for transfers between devices, shards(): ends = lax.all_to_all(edge, 'gx', split_axis=0, concat_axis=0, tiled=True)  9.96 us
    pallas_call x1, Pallas kernels, backward(): pl.pallas_call(backward_kernel, out_shape=(jax.ShapeDtypeStruct((16, 128,...  6.31 us
    all_to_all x1, starting transfers between devices, shards(): ends = lax.all_to_all(edge, 'gx', split_axis=0, concat_axis=0, tiled=True)  3.55 us
    pallas_call x1, Pallas kernels, forward(): pl.pallas_call(forward_kernel, out_shape=(jax.ShapeDtypeStruct((SLOTS, 25...  3.23 us
    pallas_call x1, Pallas kernels, pack(): pl.pallas_call(pack_kernel, out_shape=jax.ShapeDtypeStruct((DEV, 5, 4, 12...  3.04 us
  transfers between devices with their start and end apart: 1, of which 1 were waited for; matrix products, arithmetic and copies ran while one was open for 0% of the time, Pallas kernels for 0%

profile of v5, /device:TPU:0, one launch (start us, length us, event | category | flops | bytes accessed | tf_op | source)
XLA Modules:
  0.0 90.6 jit_solution(7542472889457492268)
XLA Ops:
  0.6 3.0 %pack.1 = f32[128,5,4,128]{3,2,1,0:T(4,128)} custom-call(s32[128]{0:T(128)} %bitcast.8, s32[128]{0:T(128)} %brick.1, s32[128]{0:T(128)} %fill.1, f32[128,2,256]{2,1,0:T(2,128)} %normals.1, f32[128,2,256]{2,1,0:T(2,128)} %fractions.1, s32[128,256]{1,0:T(8,128)} %offsets.1), custom_call_target="tpu_custom_call" | custom-call | tf_op jit(solution)/shard_map/pack/pallas_call | solution.py:473
  3.7 33.1 %all_to_all.15.recv = f32[128,5,4,128]{3,2,1,0:T(4,128)S(1)} all-to-all(f32[128,5,4,128]{3,2,1,0:T(4,128)} %pack.1), channel_id=1, replica_groups=mesh['gx'=16,'gy'=8] {'gx','gy'}, dimensions={0} | all-to-all | bytes 2621440 | tf_op jit(solution)/shard_map/all_to_all | solution.py:545
  36.7 0.0 copy-start
  36.8 0.0 copy-start.1
  36.8 0.0 copy-start.4
  36.8 0.0 copy-start.6
  36.8 0.0 copy-start.8
  36.8 0.0 copy-start.9
  36.8 12.2 %splat.1 = f32[8,256,128]{2,1,0:T(8,128)S(1)} custom-call(f32[128,5,4,128]{3,2,1,0:T(4,128)S(1)} %all_to_all.15.recv), custom_call_target="tpu_custom_call" | custom-call | tf_op jit(solution)/shard_map/splat/pallas_call | solution.py:486
  49.0 18.4 %all_to_all.16 = f32[8,256,128]{2,1,0:T(8,128)S(1)} all-to-all(f32[8,256,128]{2,1,0:T(8,128)S(1)} %splat.1), channel_id=1, replica_groups=mesh['gx'=16,'gy'=8] {'gy'}, dimensions={0} | all-to-all | bytes 2097152 | tf_op jit(solution)/shard_map/all_to_all | solution.py:547
  67.4 0.0 copy-done
  67.4 0.0 copy-done.1
  67.4 0.0 copy-done.4
  67.4 0.0 copy-done.6
  67.4 0.0 copy-done.8
  67.4 0.0 copy-done.9
  67.4 0.0 copy-start.2
  67.4 0.0 copy-start.3
  67.4 0.0 copy-start.5
  67.5 0.0 copy-start.7
  67.5 3.2 %forward.1 = (f32[8,256,128]{2,1,0:T(8,128)S(1)}, f32[16,3,8,256]{3,2,1,0:T(8,128)}) custom-call(f32[16,128,128]{2,1,0:T(8,128)S(1)} %bitcast.7, bf16[8,768,256]{2,1,0:T(8,128)(2,1)S(1)} %copy-done.1, bf16[256,256]{1,0:T(8,128)(2,1)S(1)} %copy-done.4, bf16[256,128]{1,0:T(8,128)(2,1)S(1)} %copy-done.6, bf16[16,256]{1,0:T(8,128)(2,1)S(1)} %copy-done.9, ...), custom_call_target="tpu_custom_call" | custom-call | tf_op jit(solution)/shard_map/forward/pallas_call | solution.py:504
  70.7 3.6 %all-to-all-start.2 = ((f32[16,3,8,256]{3,2,1,0:T(8,128)}), f32[16,3,8,256]{3,2,1,0:T(8,128)S(1)}, u32[]{:S(2)}, u32[]{:S(2)}) async-start(f32[16,3,8,256]{3,2,1,0:T(8,128)} %get-tuple-element.7), calls=%async_computation.2 | async-start | bytes 786432 | tf_op jit(solution)/shard_map/all_to_all | solution.py:549
  74.3 10.0 %all-to-all-done.2.ends = f32[16,3,8,256]{3,2,1,0:T(8,128)S(1)} async-done(((f32[16,3,8,256]{3,2,1,0:T(8,128)}), f32[16,3,8,256]{3,2,1,0:T(8,128)S(1)}, u32[]{:S(2)}, u32[]{:S(2)}) %all-to-all-start.2) | async-done | bytes 393248 | tf_op jit(solution)/shard_map/all_to_all | solution.py:549
  84.2 0.0 copy-done.2
  84.2 0.0 copy-done.3
  84.2 0.0 copy-done.5
  84.2 0.0 copy-done.7
  84.2 6.3 %backward.1 = (f32[16,128,128]{2,1,0:T(8,128)}, f32[2,16,128,128]{3,2,1,0:T(8,128)}) custom-call(s32[1]{0:T(128)} %bitcast.me, f32[8,256,128]{2,1,0:T(8,128)S(1)} %get-tuple-element.6.wave, f32[16,3,8,256]{3,2,1,0:T(8,128)S(1)} %all-to-all-done.2.ends, f32[2,16,8,256]{3,2,1,0:T(8,128)S(1)} %copy-done.2, f32[8,256,128]{2,1,0:T(8,128)S(1)} %copy-done, ...), custom_call_target="tpu_custom_call" | custom-call | tf_op jit(solution)/shard_map/backward/pallas_call | solution.py:522
Async XLA Ops:
  36.7 30.6 %copy-start = (f32[8,256,128]{2,1,0:T(8,128)S(1)}, f32[8,256,128]{2,1,0:T(8,128)}, u32[]{:S(2)}) copy-start(f32[8,256,128]{2,1,0:T(8,128)} %constant.32.clone.resp) | copy-start | bytes 3145732
  36.8 30.6 %copy-start.1 = (bf16[8,768,256]{2,1,0:T(8,128)(2,1)S(1)}, bf16[8,768,256]{2,1,0:T(8,128)(2,1)}, u32[]{:S(2)}) copy-start(bf16[8,768,256]{2,1,0:T(8,128)(2,1)} %constant.28.clone.fwd) | copy-start | bytes 9437188
  36.8 30.6 %copy-start.4 = (bf16[256,256]{1,0:T(8,128)(2,1)S(1)}, bf16[256,256]{1,0:T(8,128)(2,1)}, u32[]{:S(2)}) copy-start(bf16[256,256]{1,0:T(8,128)(2,1)} %constant.29.clone.ss) | copy-start | bytes 393220
  36.8 30.6 %copy-start.6 = (bf16[256,128]{1,0:T(8,128)(2,1)S(1)}, bf16[256,128]{1,0:T(8,128)(2,1)}, u32[]{:S(2)}) copy-start(bf16[256,128]{1,0:T(8,128)(2,1)} %constant.30.clone.s2) | copy-start | bytes 196612
  36.8 30.6 %copy-start.8 = (f32[8,1,256]{2,1,0:T(1,128)S(1)}, f32[8,1,256]{2,1,0:T(1,128)}, u32[]{:S(2)}) copy-start(f32[8,1,256]{2,1,0:T(1,128)} %constant.33.clone.nyq) | copy-start | bytes 24580
  36.8 30.6 %copy-start.9 = (bf16[16,256]{1,0:T(8,128)(2,1)S(1)}, bf16[16,256]{1,0:T(8,128)(2,1)}, u32[]{:S(2)}) copy-start(bf16[16,256]{1,0:T(8,128)(2,1)} %constant.31.clone.edges) | copy-start | bytes 24580
  67.4 16.8 %copy-start.2 = (f32[2,16,8,256]{3,2,1,0:T(8,128)S(1)}, f32[2,16,8,256]{3,2,1,0:T(8,128)}, u32[]{:S(2)}) copy-start(f32[2,16,8,256]{3,2,1,0:T(8,128)} %constant.34.clone.link) | copy-start | bytes 786436
  67.4 16.8 %copy-start.3 = (bf16[256,256]{1,0:T(8,128)(2,1)S(1)}, bf16[256,256]{1,0:T(8,128)(2,1)}, u32[]{:S(2)}) copy-start(bf16[256,256]{1,0:T(8,128)(2,1)} %constant.36.clone.back1) | copy-start | bytes 393220
  67.4 16.8 %copy-start.5 = (bf16[128,256]{1,0:T(8,128)(2,1)S(1)}, bf16[128,256]{1,0:T(8,128)(2,1)}, u32[]{:S(2)}) copy-start(bf16[128,256]{1,0:T(8,128)(2,1)} %constant.37.clone.back2) | copy-start | bytes 196612
  67.5 16.8 %copy-start.7 = (bf16[16,384]{1,0:T(8,128)(2,1)S(1)}, bf16[16,384]{1,0:T(8,128)(2,1)}, u32[]{:S(2)}) copy-start(bf16[16,384]{1,0:T(8,128)(2,1)} %constant.35.clone.ranks) | copy-start | bytes 36868
  70.7 13.5 %all-to-all-start.2 = ((f32[16,3,8,256]{3,2,1,0:T(8,128)}), f32[16,3,8,256]{3,2,1,0:T(8,128)S(1)}, u32[]{:S(2)}, u32[]{:S(2)}) async-start(f32[16,3,8,256]{3,2,1,0:T(8,128)} %get-tuple-element.7), calls=%async_computation.2 | async-start | bytes 786432 | tf_op jit(solution)/shard_map/all_to_all | solution.py:549

commit v6 on v5

--- a/solution.py
+++ b/solution.py
@@ -428,28 +428,28 @@
     ind, grad_x, grad_y = parts_all.at[0], parts_all.at[1], parts_all.at[2]
     for c in reversed(range(CHUNKS)):
 
-        def radix(t, carry):
-            start = c * chunk + t * step
-            rows = pl.ds(pl.multiple_of(start, step), step)
-            far_rows = pl.ds(pl.multiple_of(128 + start, step), step)
-            for part in range(2):
-                lanes = slice(128 * part, 128 * part + 128)
+        rows_out = pl.ds(c * chunk, chunk)
+        for part in range(2):
+            lanes = slice(128 * part, 128 * part + 128)
+
+            def radix(t, carry):
+                start = c * chunk + t * step
+                rows = pl.ds(pl.multiple_of(start, step), step)
+                far_rows = pl.ds(pl.multiple_of(128 + start, step), step)
                 values = radix_inverse(
                     [(hs[s, rows, lanes], hs[s, far_rows, lanes]) for s in range(SLOTS)]
                 )
                 for a in range(16):
                     parts_all[part, a, rows, :] = values[a]
-            return carry
-
-        lax.fori_loop(0, chunk // step, radix, 0, unroll=RADIX_UNROLL)
-        rows = pl.ds(c * chunk, chunk)
-        send(0, rows)
-        send(1, rows)
+                return carry
+
+            lax.fori_loop(0, chunk // step, radix, 0, unroll=RADIX_UNROLL)
+            send(part, rows_out)
         low, high = c * chunk, min((c + 1) * chunk, 127)
         for a in range(16):
             grad_y[a, low:high, :] = ind[a, low + 1 : high + 1, :] - ind[a, low:high, :]
         if c < CHUNKS - 1:
-            send(2, rows)
+            send(2, rows_out)
     for a in range(16):
         grad_y[a, 127:128, :] = ind[(a + 1) % 16, 0:1, :] - ind[a, 127:128, :]
     send(2, pl.ds(128 - chunk, chunk))

time: 90.9 us -> 90.9 us (level)
  no operation moved by 1% of the time
where the time goes in v6:
time: 90.9 us; the launch traced here: 90.5 us
  blocking collectives  51.5 us (57%)
  Pallas kernels  24.7 us (27%)
  waiting for transfers between devices  9.96 us (11%)
  starting transfers between devices  3.55 us (4%)
    all_to_all x1, blocking collectives, shards(): lax.all_to_all(send, ('gx', 'gy'), split_axis=0, concat_axis=0, tiled=True)  33.1 us
    all_to_all x1, blocking collectives, shards(): plane = lax.all_to_all(tile, 'gy', split_axis=0, concat_axis=0, tiled=True)  18.4 us
    pallas_call x1, Pallas kernels, splat(): pl.pallas_call(splat_kernel, out_shape=jax.ShapeDtypeStruct((Z, NY // GY,...  12.2 us
    all_to_all x1, waiting for transfers between devices, shards(): ends = lax.all_to_all(edge, 'gx', split_axis=0, concat_axis=0, tiled=True)  9.96 us
    pallas_call x1, Pallas kernels, backward(): pl.pallas_call(backward_kernel, out_shape=(jax.ShapeDtypeStruct((16, 128,...  6.26 us
    all_to_all x1, starting transfers between devices, shards(): ends = lax.all_to_all(edge, 'gx', split_axis=0, concat_axis=0, tiled=True)  3.55 us
    pallas_call x1, Pallas kernels, forward(): pl.pallas_call(forward_kernel, out_shape=(jax.ShapeDtypeStruct((SLOTS, 25...  3.23 us
    pallas_call x1, Pallas kernels, pack(): pl.pallas_call(pack_kernel, out_shape=jax.ShapeDtypeStruct((DEV, 5, 4, 12...  3.04 us
  transfers between devices with their start and end apart: 1, of which 1 were waited for; matrix products, arithmetic and copies ran while one was open for 0% of the time, Pallas kernels for 0%

profile of v6, /device:TPU:0, one launch (start us, length us, event | category | flops | bytes accessed | tf_op | source)
XLA Modules:
  0.0 90.5 jit_solution(5757053666268151155)
XLA Ops:
  0.6 3.0 %pack.1 = f32[128,5,4,128]{3,2,1,0:T(4,128)} custom-call(s32[128]{0:T(128)} %bitcast.8, s32[128]{0:T(128)} %brick.1, s32[128]{0:T(128)} %fill.1, f32[128,2,256]{2,1,0:T(2,128)} %normals.1, f32[128,2,256]{2,1,0:T(2,128)} %fractions.1, s32[128,256]{1,0:T(8,128)} %offsets.1), custom_call_target="tpu_custom_call" | custom-call | tf_op jit(solution)/shard_map/pack/pallas_call | solution.py:473
  3.7 33.1 %all_to_all.15.recv = f32[128,5,4,128]{3,2,1,0:T(4,128)S(1)} all-to-all(f32[128,5,4,128]{3,2,1,0:T(4,128)} %pack.1), channel_id=1, replica_groups=mesh['gx'=16,'gy'=8] {'gx','gy'}, dimensions={0} | all-to-all | bytes 2621440 | tf_op jit(solution)/shard_map/all_to_all | solution.py:545
  36.7 0.0 copy-start
  36.8 0.0 copy-start.1
  36.8 0.0 copy-start.4
  36.8 0.0 copy-start.6
  36.8 0.0 copy-start.8
  36.8 0.0 copy-start.9
  36.8 12.2 %splat.1 = f32[8,256,128]{2,1,0:T(8,128)S(1)} custom-call(f32[128,5,4,128]{3,2,1,0:T(4,128)S(1)} %all_to_all.15.recv), custom_call_target="tpu_custom_call" | custom-call | tf_op jit(solution)/shard_map/splat/pallas_call | solution.py:486
  49.0 18.4 %all_to_all.16 = f32[8,256,128]{2,1,0:T(8,128)S(1)} all-to-all(f32[8,256,128]{2,1,0:T(8,128)S(1)} %splat.1), channel_id=1, replica_groups=mesh['gx'=16,'gy'=8] {'gy'}, dimensions={0} | all-to-all | bytes 2097152 | tf_op jit(solution)/shard_map/all_to_all | solution.py:547
  67.4 0.0 copy-done
  67.4 0.0 copy-done.1
  67.4 0.0 copy-done.4
  67.4 0.0 copy-done.6
  67.4 0.0 copy-done.8
  67.4 0.0 copy-done.9
  67.4 0.0 copy-start.2
  67.4 0.0 copy-start.3
  67.4 0.0 copy-start.5
  67.5 0.0 copy-start.7
  67.5 3.2 %forward.1 = (f32[8,256,128]{2,1,0:T(8,128)S(1)}, f32[16,3,8,256]{3,2,1,0:T(8,128)}) custom-call(f32[16,128,128]{2,1,0:T(8,128)S(1)} %bitcast.7, bf16[8,768,256]{2,1,0:T(8,128)(2,1)S(1)} %copy-done.1, bf16[256,256]{1,0:T(8,128)(2,1)S(1)} %copy-done.4, bf16[256,128]{1,0:T(8,128)(2,1)S(1)} %copy-done.6, bf16[16,256]{1,0:T(8,128)(2,1)S(1)} %copy-done.9, ...), custom_call_target="tpu_custom_call" | custom-call | tf_op jit(solution)/shard_map/forward/pallas_call | solution.py:504
  70.7 3.6 %all-to-all-start.2 = ((f32[16,3,8,256]{3,2,1,0:T(8,128)}), f32[16,3,8,256]{3,2,1,0:T(8,128)S(1)}, u32[]{:S(2)}, u32[]{:S(2)}) async-start(f32[16,3,8,256]{3,2,1,0:T(8,128)} %get-tuple-element.7), calls=%async_computation.2 | async-start | bytes 786432 | tf_op jit(solution)/shard_map/all_to_all | solution.py:549
  74.3 10.0 %all-to-all-done.2.ends = f32[16,3,8,256]{3,2,1,0:T(8,128)S(1)} async-done(((f32[16,3,8,256]{3,2,1,0:T(8,128)}), f32[16,3,8,256]{3,2,1,0:T(8,128)S(1)}, u32[]{:S(2)}, u32[]{:S(2)}) %all-to-all-start.2) | async-done | bytes 393248 | tf_op jit(solution)/shard_map/all_to_all | solution.py:549
  84.2 0.0 copy-done.2
  84.2 0.0 copy-done.3
  84.2 0.0 copy-done.5
  84.2 0.0 copy-done.7
  84.2 6.3 %backward.1 = (f32[16,128,128]{2,1,0:T(8,128)}, f32[2,16,128,128]{3,2,1,0:T(8,128)}) custom-call(s32[1]{0:T(128)} %bitcast.me, f32[8,256,128]{2,1,0:T(8,128)S(1)} %get-tuple-element.6.wave, f32[16,3,8,256]{3,2,1,0:T(8,128)S(1)} %all-to-all-done.2.ends, f32[2,16,8,256]{3,2,1,0:T(8,128)S(1)} %copy-done.2, f32[8,256,128]{2,1,0:T(8,128)S(1)} %copy-done, ...), custom_call_target="tpu_custom_call" | custom-call | tf_op jit(solution)/shard_map/backward/pallas_call | solution.py:522
Async XLA Ops:
  36.7 30.6 %copy-start = (f32[8,256,128]{2,1,0:T(8,128)S(1)}, f32[8,256,128]{2,1,0:T(8,128)}, u32[]{:S(2)}) copy-start(f32[8,256,128]{2,1,0:T(8,128)} %constant.32.clone.resp) | copy-start | bytes 3145732
  36.8 30.6 %copy-start.1 = (bf16[8,768,256]{2,1,0:T(8,128)(2,1)S(1)}, bf16[8,768,256]{2,1,0:T(8,128)(2,1)}, u32[]{:S(2)}) copy-start(bf16[8,768,256]{2,1,0:T(8,128)(2,1)} %constant.28.clone.fwd) | copy-start | bytes 9437188
  36.8 30.6 %copy-start.4 = (bf16[256,256]{1,0:T(8,128)(2,1)S(1)}, bf16[256,256]{1,0:T(8,128)(2,1)}, u32[]{:S(2)}) copy-start(bf16[256,256]{1,0:T(8,128)(2,1)} %constant.29.clone.ss) | copy-start | bytes 393220
  36.8 30.6 %copy-start.6 = (bf16[256,128]{1,0:T(8,128)(2,1)S(1)}, bf16[256,128]{1,0:T(8,128)(2,1)}, u32[]{:S(2)}) copy-start(bf16[256,128]{1,0:T(8,128)(2,1)} %constant.30.clone.s2) | copy-start | bytes 196612
  36.8 30.6 %copy-start.8 = (f32[8,1,256]{2,1,0:T(1,128)S(1)}, f32[8,1,256]{2,1,0:T(1,128)}, u32[]{:S(2)}) copy-start(f32[8,1,256]{2,1,0:T(1,128)} %constant.33.clone.nyq) | copy-start | bytes 24580
  36.8 30.6 %copy-start.9 = (bf16[16,256]{1,0:T(8,128)(2,1)S(1)}, bf16[16,256]{1,0:T(8,128)(2,1)}, u32[]{:S(2)}) copy-start(bf16[16,256]{1,0:T(8,128)(2,1)} %constant.31.clone.edges) | copy-start | bytes 24580
  67.4 16.8 %copy-start.2 = (f32[2,16,8,256]{3,2,1,0:T(8,128)S(1)}, f32[2,16,8,256]{3,2,1,0:T(8,128)}, u32[]{:S(2)}) copy-start(f32[2,16,8,256]{3,2,1,0:T(8,128)} %constant.34.clone.link) | copy-start | bytes 786436
  67.4 16.8 %copy-start.3 = (bf16[256,256]{1,0:T(8,128)(2,1)S(1)}, bf16[256,256]{1,0:T(8,128)(2,1)}, u32[]{:S(2)}) copy-start(bf16[256,256]{1,0:T(8,128)(2,1)} %constant.36.clone.back1) | copy-start | bytes 393220
  67.4 16.8 %copy-start.5 = (bf16[128,256]{1,0:T(8,128)(2,1)S(1)}, bf16[128,256]{1,0:T(8,128)(2,1)}, u32[]{:S(2)}) copy-start(bf16[128,256]{1,0:T(8,128)(2,1)} %constant.37.clone.back2) | copy-start | bytes 196612
  67.5 16.8 %copy-start.7 = (bf16[16,384]{1,0:T(8,128)(2,1)S(1)}, bf16[16,384]{1,0:T(8,128)(2,1)}, u32[]{:S(2)}) copy-start(bf16[16,384]{1,0:T(8,128)(2,1)} %constant.35.clone.ranks) | copy-start | bytes 36868
  70.7 13.5 %all-to-all-start.2 = ((f32[16,3,8,256]{3,2,1,0:T(8,128)}), f32[16,3,8,256]{3,2,1,0:T(8,128)S(1)}, u32[]{:S(2)}, u32[]{:S(2)}) async-start(f32[16,3,8,256]{3,2,1,0:T(8,128)} %get-tuple-element.7), calls=%async_computation.2 | async-start | bytes 786432 | tf_op jit(solution)/shard_map/all_to_all | solution.py:549
